TPU v7x, 32 devices: a whole 2x2x4 slice. The times are simulated.
32 devices in a mesh: row: 8 (over y, x, core), col: 4 (over z).
Axes of the slice: x: 2, y: 2, z: 4, core: 2. Of those that a mesh axis runs over, the one named last changes fastest.
Arguments:
- vector: float32 [4096, 4096], P('row', 'col'), may hold values from -6 to 6
- one_electron: float32 [16, 16], replicated, may hold values from -0.18 to 0.18
- links: int32 [32, 8], replicated, may hold values from 0 to 31, as said below
- counts: int32 [32], replicated, may hold values from 4 to 8, as said below
- pairs: int32 [32, 8], P('row'), may hold values from 0 to 255
- signs: int32 [32, 8, 128, 128], P('row'), may hold values from -1 to 1
Outputs:
- sigma_vector: float32 [4096, 4096], P('row', 'col')
Inputs may be any that keep to these rules, and one draw needn't show every extreme that they name: `links`: entries name string blocks; only the first counts[I] entries of block I are used. Counting used entries only, the blocks I with I // 4 = d name blocks K with K // 4 = s at most 4 times for any d and s, and some pair d, s reaches 4. Block I has counts[I] used links; every block I with I % 4 = 0 has 8.
All inputs are finite; a program needn't handle non-finite values.
Results may differ from a plain program's by a relative error of at most 0.000051.
Values sent between devices are 32-bit elements; how exact they have to be, the bound alone decides.
A program may use at most 128 MiB of HBM per device.

v0:
```python
import functools

import jax
import jax.numpy as jnp
from jax import lax
from jax.experimental import pallas as pl
from jax.experimental.pallas import tpu as pltpu
from jax.sharding import PartitionSpec as P

MESH = pl.DeviceIdType.MESH
PARTS_A = 4
PARTS_B = 4
PAD = 8
PIECES = 4


def pair_values(pair_ids, used, integrals):
    flat_table = integrals.reshape(-1)
    onehot = pair_ids[:, :, None] == jnp.arange(flat_table.shape[0], dtype=jnp.int32)[None, None, :]
    values = jnp.sum(jnp.where(onehot, flat_table[None, None, :], 0.0), axis=2)
    in_use = jnp.arange(pair_ids.shape[1], dtype=jnp.int32)[None, :] < used[:, None]
    return jnp.where(in_use, values, 0.0)


def split(value):
    high = value.astype(jnp.bfloat16)
    low = (value - high.astype(jnp.float32)).astype(jnp.bfloat16)
    return high, low


def kernel(rows, cols, blocks, link_max, links, v, tab, out, *scratch):
    scratch = list(scratch)
    colbuf = [scratch.pop(0) for _ in range(PARTS_A)]
    rowbuf = [scratch.pop(0) for _ in range(PARTS_B)]
    own_tab, beta_tab, help_tab, alpha_signs, beta_signs, help_signs, shared = scratch[:7]
    asend, arecv, bsend, brecv, tsend, trecv, hsend, hrecv, rsend, rrecv, lsem = scratch[7:]

    size = own_tab.shape[2]
    width = out.shape[1]
    wide = width // PARTS_A
    tall = out.shape[0] // PARTS_B
    spread = rows // cols
    blocks_b = blocks * spread
    tables = blocks * link_max
    chips = rows // 2
    reach = chips // 2
    across = chips // 2
    helped = PARTS_B // 2 if cols >= 4 else 0

    r = lax.axis_index("row")
    c = lax.axis_index("col")
    core = lax.rem(r, 2)
    chip = r // 2
    other = r + 1 - 2 * core
    place = jnp.where(chip < across, chip, chips - 1 - (chip - across))

    def chip_at(position):
        position = lax.rem(position + 2 * chips, chips)
        return jnp.where(position < across, position, across + (chips - 1 - position))

    def row_at(position, k):
        return 2 * chip_at(position) + k

    right = (row_at(place + 1, core), c)
    left = (row_at(place - 1, core), c)
    partner = (other, c)
    up = (r, jnp.minimum(c + 1, cols - 1))
    down = (r, jnp.maximum(c - 1, 0))
    has_up = c < cols - 1
    has_down = c > 0
    at_end = (c == 0) | (c == cols - 1)
    inner = jnp.logical_not(at_end)
    helper = (c == 1) | (c == cols - 2)
    aided = jnp.where(c == 1, 0, cols - 1)
    inward = jnp.where(c == 0, 1, cols - 2)

    barrier = pltpu.get_barrier_semaphore()
    for device in (right, left, partner):
        pl.semaphore_signal(barrier, inc=1, device_id=device, device_id_type=MESH)

    @pl.when(has_up)
    def _():
        pl.semaphore_signal(barrier, inc=1, device_id=up, device_id_type=MESH)

    @pl.when(has_down)
    def _():
        pl.semaphore_signal(barrier, inc=1, device_id=down, device_id_type=MESH)

    loads = []
    for j in range(PARTS_A):
        for i in range(blocks):
            loads.append(pltpu.make_async_copy(
                v.at[pl.ds(i * size, size), pl.ds(j * wide, wide)],
                colbuf[j].at[r * blocks + i], lsem.at[len(loads)]))
    for i in range(PARTS_B):
        for k in range(blocks_b):
            loads.append(pltpu.make_async_copy(
                v.at[pl.ds(i * tall, tall), pl.ds(k * size, size)],
                rowbuf[i].at[c * blocks_b + k], lsem.at[len(loads)]))
    loads.append(pltpu.make_async_copy(tab, own_tab, lsem.at[len(loads)]))
    for load in loads:
        load.start()
    for load in loads:
        load.wait()

    pl.semaphore_wait(barrier, 3 + has_up.astype(jnp.int32) + has_down.astype(jnp.int32))

    pending = []

    def send(src, dst, ssem, rsem, device, cond=None):
        copy = pltpu.make_async_remote_copy(
            src_ref=src, dst_ref=dst, send_sem=ssem, recv_sem=rsem,
            device_id=device, device_id_type=MESH)
        pending.append((cond, copy))
        if cond is None:
            copy.start()
        else:
            pl.when(cond)(copy.start)

    def arrive(ref, ssem, rsem, cond=None):
        copy = pltpu.make_async_remote_copy(
            src_ref=ref, dst_ref=ref, send_sem=ssem, recv_sem=rsem,
            device_id=partner, device_id_type=MESH)
        if cond is None:
            copy.wait_recv()
        else:
            pl.when(cond)(copy.wait_recv)

    def alpha_part(j, position, k, t, leftward):
        start = row_at(position, k) * blocks
        count = blocks
        if t == reach - 1:
            count = blocks // 2
            if leftward:
                start = start + count
        return colbuf[j].at[pl.ds(start, count)]

    def alpha_send(j, t):
        ref = alpha_part(j, place - t, core, t, False)
        send(ref, ref, asend.at[j, t], arecv.at[j, t], right)
        ref = alpha_part(j, place + t, core, t, True)
        send(ref, ref, asend.at[j, reach + t], arecv.at[j, reach + t], left)

    def alpha_arrive(j, t):
        m = chips + 1 + t
        ref = alpha_part(j, place - 1 - t, core, t, False)
        arrive(ref, asend.at[j, t], arecv.at[j, t])
        send(ref, ref, asend.at[j, m], arecv.at[j, m], partner)
        m = m + reach
        ref = alpha_part(j, place + 1 + t, core, t, True)
        arrive(ref, asend.at[j, reach + t], arecv.at[j, reach + t])
        send(ref, ref, asend.at[j, m], arecv.at[j, m], partner)

    def alpha_partner(j):
        m = chips
        ref = colbuf[j].at[pl.ds(other * blocks, blocks)]
        arrive(ref, asend.at[j, m], arecv.at[j, m])
        for t in range(reach):
            m = chips + 1 + t
            arrive(alpha_part(j, place - 1 - t, 1 - core, t, False), asend.at[j, m], arecv.at[j, m])
            m = m + reach
            arrive(alpha_part(j, place + 1 + t, 1 - core, t, True), asend.at[j, m], arecv.at[j, m])

    def beta_part(i, tile):
        return rowbuf[i].at[pl.ds(jnp.clip(tile, 0, cols - 1) * blocks_b, blocks_b)]

    def in_turn(i, tile, late):
        if i < helped or helped == 0:
            return jnp.bool_(not late) & (tile >= 0) & (tile < cols)
        from_end = (tile == 0) | (tile == cols - 1)
        return from_end if late else (tile > 0) & (tile < cols - 1)

    def beta_send(i, t, late):
        if late and (i < helped or helped == 0):
            return
        above = has_up & in_turn(i, c - t, late)
        below = has_down & in_turn(i, c + t, late)
        if i < helped:
            above = above & (c + 1 < cols - 1)
            below = below & (c - 1 > 0)
        ref = beta_part(i, c - t)
        m = 2 * late * (cols - 1) + t
        send(ref, ref, bsend.at[i, m], brecv.at[i, m], up, above)
        ref = beta_part(i, c + t)
        m = m + cols - 1
        send(ref, ref, bsend.at[i, m], brecv.at[i, m], down, below)

    def beta_arrive(i, t, late):
        if late and (i < helped or helped == 0):
            return
        above = in_turn(i, c - 1 - t, late)
        below = in_turn(i, c + 1 + t, late)
        if i < helped:
            above = above & inner
            below = below & inner
        m = 2 * late * (cols - 1) + t
        arrive(beta_part(i, c - 1 - t), bsend.at[i, m], brecv.at[i, m], above)
        m = m + cols - 1
        arrive(beta_part(i, c + 1 + t), bsend.at[i, m], brecv.at[i, m], below)

    def table_places(s):
        source = c * spread + s
        source_chip = source // 2
        source_place = jnp.where(
            source_chip < across, source_chip, chips - 1 - (source_chip - across))
        distance = lax.rem(place - source_place + chips, chips)
        return lax.rem(source, 2), distance

    piece = tables // (2 * PIECES)

    def table_stage(s, q, d):
        source_core, distance = table_places(s)
        for h in range(2):
            hops = distance if h == 0 else lax.rem(chips - distance, chips)
            here = (core == source_core) & (hops == d)
            part = pl.ds((h * PIECES + q) * piece, piece)
            ref = beta_tab.at[s, part]
            src = ref if d else own_tab.at[part]
            if d:
                arrive(ref, tsend.at[s, h, q, 0], trecv.at[s, h, q], here)
            if d + 1 < chips:
                send(src, ref, tsend.at[s, h, q, 0], trecv.at[s, h, q],
                     right if h == 0 else left, here)
            send(src, ref, tsend.at[s, h, q, 1], trecv.at[s, h, q], partner, here)

    def table_finish(s):
        source_core, distance = table_places(s)
        mine = core == source_core
        for q in range(PIECES):
            for h in range(2):
                ref = beta_tab.at[s, pl.ds((h * PIECES + q) * piece, piece)]
                arrive(ref, tsend.at[s, h, q, 0], trecv.at[s, h, q], jnp.logical_not(mine))

        @pl.when(mine & (distance == 0))
        def _():
            copy = pltpu.make_async_copy(own_tab, beta_tab.at[s], lsem.at[0])
            copy.start()
            copy.wait()

    half = tables // 2

    def help_send(s):
        for h in range(2):
            ref = pl.ds(h * half, half)
            send(beta_tab.at[s, ref], help_tab.at[s, ref], hsend.at[s, h, 0], hrecv.at[s, h],
                 (r, inward), at_end & (core == s % 2))

    def help_arrive(s):
        for h in range(2):
            ref = help_tab.at[s, pl.ds(h * half, half)]
            arrive(ref, hsend.at[s, h, 1], hrecv.at[s, h], helper & (core == s % 2))
            send(ref, ref, hsend.at[s, h, 1], hrecv.at[s, h], partner, helper & (core == s % 2))

    def help_finish(s):
        for h in range(2):
            ref = help_tab.at[s, pl.ds(h * half, half)]
            arrive(ref, hsend.at[s, h, 1], hrecv.at[s, h], helper & (core != s % 2))

    def shared_part(i):
        return shared.at[pl.ds(i * tall, tall)]

    def widen(source, target):
        for s in range(spread):
            @pl.loop(0, tables)
            def _(index):
                signs = source[s, index, :size, :].astype(jnp.bfloat16)
                target[s * tables + index] = jnp.concatenate([signs, signs], axis=1)

    for s in range(spread):
        for q in range(PIECES):
            table_stage(s, q, 0)
    for j in range(PARTS_A):
        alpha_send(j, 0)
        ref = colbuf[j].at[pl.ds(r * blocks, blocks)]
        send(ref, ref, asend.at[j, chips], arecv.at[j, chips], partner)
        if j == 0:
            for i in range(PARTS_B):
                beta_send(i, 0, 0)
                beta_send(i, 0, 1)
            for wave in range(PIECES + chips - 2):
                for q in range(PIECES):
                    if 1 <= wave - q + 1 < chips:
                        for s in range(spread):
                            table_stage(s, q, wave - q + 1)

    out[...] = jnp.zeros_like(out)

    @pl.loop(0, tables)
    def _(index):
        signs = own_tab[index, :size, :].astype(jnp.bfloat16)
        alpha_signs[index] = jnp.concatenate([signs, signs], axis=1)

    def alpha_compute(j):
        @pl.loop(0, blocks)
        def _(block):
            total = jnp.zeros((size, wide), jnp.float32)
            for l in range(link_max):
                source = links[r * blocks + block, l]
                high, low = split(colbuf[j][source])
                index = block * link_max + l
                term = jnp.dot(alpha_signs[index], jnp.concatenate([high, low], axis=0),
                               preferred_element_type=jnp.float32)
                scale = own_tab[index, pl.ds(size, 1), :]
                scale = jnp.concatenate([scale] * (wide // size), axis=1)
                total = total + term * scale
            where = (pl.ds(pl.multiple_of(block * size, size), size), pl.ds(j * wide, wide))
            out[where] = out[where] + total

    def beta_compute(i, owner, tabs, signs, target, add):
        @pl.loop(0, blocks_b)
        def _(block):
            total = jnp.zeros((tall, size), jnp.float32)
            for l in range(link_max):
                source = links[owner * blocks_b + block, l]
                high, low = split(rowbuf[i][source])
                index = block * link_max + l
                term = lax.dot_general(
                    jnp.concatenate([high, low], axis=1), signs[index],
                    (((1,), (1,)), ((), ())), preferred_element_type=jnp.float32)
                scale = tabs[block // blocks, lax.rem(index, tables), pl.ds(size, 1), :]
                total = total + term * scale
            where = (pl.ds(i * tall, tall), pl.ds(pl.multiple_of(block * size, size), size))
            if add:
                total = target[where] + total
            target[where] = total

    for s in range(spread):
        table_finish(s)
    if helped:
        for s in range(spread):
            help_send(s)
    widen(beta_tab, beta_signs)

    for t in range(cols - 1):
        for i in range(PARTS_B):
            beta_arrive(i, t, 0)
            if t < cols - 2:
                beta_send(i, t + 1, 0)
        if t < reach - 1:
            for j in range(PARTS_A):
                alpha_arrive(j, t)
                alpha_send(j, t + 1)
    for t in range(cols - 1, reach - 1):
        for j in range(PARTS_A):
            alpha_arrive(j, t)
            alpha_send(j, t + 1)

    def own_helped(add):
        for i in range(helped):
            @pl.when(inner)
            def _():
                beta_compute(i, c, beta_tab, beta_signs, out, add)

    for i in range(helped, PARTS_B):
        beta_arrive(i, 0, 1)
        beta_send(i, 1, 1)
    own_helped(True)
    for t in range(1, cols - 2):
        for i in range(helped, PARTS_B):
            beta_arrive(i, t, 1)
            beta_send(i, t + 1, 1)
    if helped:
        for s in range(spread):
            help_arrive(s)
        for s in range(spread):
            help_finish(s)

        @pl.when(helper)
        def _():
            widen(help_tab, help_signs)

        for i in range(helped):
            @pl.when(helper)
            def _():
                beta_compute(i, aided, help_tab, help_signs, shared, False)

            send(shared_part(i), shared_part(i), rsend.at[i], rrecv.at[i], (r, aided), helper)

    for j in range(PARTS_A):
        alpha_arrive(j, reach - 1)
        alpha_partner(j)
        alpha_compute(j)
    for i in range(helped):
        arrive(shared_part(i), rsend.at[i], rrecv.at[i], at_end)

        @pl.when(at_end)
        def _():
            rows_here = pl.ds(i * tall, tall)
            out[rows_here, :] = out[rows_here, :] + shared[rows_here, :]

    for i in range(helped, PARTS_B):
        beta_arrive(i, cols - 2, 1)
        beta_compute(i, c, beta_tab, beta_signs, out, True)

    for cond, copy in pending:
        if cond is None:
            copy.wait_send()
        else:
            pl.when(cond)(copy.wait_send)


def local(vector, one_electron, links, counts, pairs, signs, rows, cols):
    blocks, link_max = pairs.shape
    size = signs.shape[2]
    high, width = vector.shape
    spread = rows // cols
    tables = blocks * link_max
    used = lax.dynamic_slice_in_dim(counts, lax.axis_index("row") * blocks, blocks)
    coef = pair_values(pairs, used, one_electron).reshape(tables, 1, 1)
    tab = jnp.concatenate(
        [signs.reshape(tables, size, size).astype(jnp.float32),
         jnp.broadcast_to(coef, (tables, PAD, size))], axis=1)
    chips = rows // 2
    scratch = [pltpu.VMEM((rows * blocks, size, width // PARTS_A), jnp.float32)] * PARTS_A
    scratch += [pltpu.VMEM((cols * blocks * spread, high // PARTS_B, size), jnp.float32)] * PARTS_B
    scratch += [
        pltpu.VMEM((tables, size + PAD, size), jnp.float32),
        pltpu.VMEM((spread, tables, size + PAD, size), jnp.float32),
        pltpu.VMEM((spread, tables, size + PAD, size), jnp.float32),
        pltpu.VMEM((tables, size, 2 * size), jnp.bfloat16),
        pltpu.VMEM((spread * tables, size, 2 * size), jnp.bfloat16),
        pltpu.VMEM((spread * tables, size, 2 * size), jnp.bfloat16),
        pltpu.VMEM((high // 2, width), jnp.float32),
        pltpu.SemaphoreType.DMA((PARTS_A, 2 * chips + 1)),
        pltpu.SemaphoreType.DMA((PARTS_A, 2 * chips + 1)),
        pltpu.SemaphoreType.DMA((PARTS_B, 4 * cols - 4)),
        pltpu.SemaphoreType.DMA((PARTS_B, 4 * cols - 4)),
        pltpu.SemaphoreType.DMA((spread, 2, PIECES, 2)),
        pltpu.SemaphoreType.DMA((spread, 2, PIECES)),
        pltpu.SemaphoreType.DMA((spread, 2, 2)),
        pltpu.SemaphoreType.DMA((spread, 2)),
        pltpu.SemaphoreType.DMA((PARTS_B,)),
        pltpu.SemaphoreType.DMA((PARTS_B,)),
        pltpu.SemaphoreType.DMA((PARTS_A * blocks + PARTS_B * blocks * spread + 1,)),
    ]
    return pl.pallas_call(
        functools.partial(kernel, rows, cols, blocks, link_max),
        out_shape=jax.ShapeDtypeStruct(vector.shape, jnp.float32),
        in_specs=[
            pl.BlockSpec(memory_space=pltpu.SMEM),
            pl.BlockSpec(memory_space=pl.ANY),
            pl.BlockSpec(memory_space=pl.ANY),
        ],
        out_specs=pl.BlockSpec(memory_space=pltpu.VMEM),
        scratch_shapes=scratch,
        compiler_params=pltpu.CompilerParams(
            collective_id=0, has_side_effects=True, vmem_limit_bytes=60 << 20),
    )(links, vector, tab)


def solution(mesh):
    in_specs = (P("row", "col"), P(), P(), P(), P("row", None), P("row", None, None, None))
    out_specs = P("row", "col")
    body = functools.partial(local, rows=mesh.shape["row"], cols=mesh.shape["col"])
    return jax.shard_map(body, mesh=mesh, in_specs=in_specs, out_specs=out_specs, check_vma=False)
```

profile of v0, /device:TPU:0, one launch (start us, length us, event | category | flops | bytes accessed | tf_op | source)
XLA Modules:
  0.0 159.5 jit_solution(11074984708017093249)
XLA Ops:
  0.0 0.7 dynamic_slice.3
  0.7 0.8 broadcast_in_dim.27
  1.5 0.8 select_reduce_fusion
  2.3 0.1 fusion
  2.4 0.1 select_n.21
  2.5 0.1 broadcast_in_dim.31
  2.6 1.7 %convert_element_type.6 = f32[4,8,128,128]{3,2,1,0:T(8,128)S(1)} convert(s32[4,8,128,128]{3,2,1,0:T(8,128)} %param.11) | non-fusion elementwise | flops 524288 | bytes 4194304 | tf_op jit(solution)/shard_map/convert_element_type | solution.py:411
  4.3 0.0 copy-start
  4.4 1.6 pad_maximum_fusion.tab
  5.9 0.0 copy-done
  5.9 0.7 copy.8.links
  6.6 149.7 %shard_map.64 = f32[512,1024]{1,0:T(8,128)} custom-call(s32[32,8]{1,0:T(8,128)} %copy.8.links, f32[512,1024]{1,0:T(8,128)} %v.1, f32[32,136,128]{2,1,0:T(8,128)} %pad_maximum_fusion.tab), custom_call_target="tpu_custom_call" | custom-call | tf_op jit(solution)/shard_map/pallas_call | solution.py:436
  156.3 3.2 %copy.10 = f32[512,1024]{1,0:T(8,128)} copy(f32[512,1024]{1,0:T(8,128)} %shard_map.64) | data formatting | bytes 4194304
Async XLA Ops:
  4.3 1.6 copy-start
where the time goes:
time: 160 us; the launch traced here: 159 us
  Pallas kernels  150 us (94%)
  local copies, waits for them, and re-layouts  5.53 us (3%)
  other arithmetic  4.21 us (3%)
    pallas_call x1, Pallas kernels, local(): pl.pallas_call(functools.partial(kernel, rows, cols, blocks, link_max), o...  150 us
    unnamed x4, local copies, waits for them, and re-layouts  3.85 us

commit v1 on v0

v1 whole, which is shorter than its diff:
```python
import functools

import jax
import jax.numpy as jnp
from jax import lax
from jax.experimental import pallas as pl
from jax.experimental.pallas import tpu as pltpu
from jax.sharding import PartitionSpec as P

MESH = pl.DeviceIdType.MESH
PARTS_A = 4
PIECES = 4
EARLY = 2
TILE = 45.0
HOP = 1.5
PIECE = 5.6


def split(value):
    high = value.astype(jnp.bfloat16)
    low = (value - high.astype(jnp.float32)).astype(jnp.bfloat16)
    return high, low


def row_parts(high, cols):
    helps = cols >= 4
    quarter, eighth, last = high // 4, high // 8, high // 16
    return [(quarter, False), (quarter, False), (quarter, helps), (eighth, helps), (last, helps), (last, helps)]


def row_chunks(high, cols):
    chunks, first = [], 0
    for part, (height, helped) in enumerate(row_parts(high, cols)):
        piece = min(height, high // 8)
        for offset in range(0, height, piece):
            chunks.append((part, offset, piece, first + offset, helped))
        first += height
    return chunks


def kernel(rows, cols, blocks, link_max, links, counts, integrals, pairs, v, tab, out, *scratch):
    size = tab.shape[1]
    high, width = out.shape
    parts = row_parts(high, cols)
    chunks = row_chunks(high, cols)
    firsts = [sum(p[0] for p in parts[:i]) for i in range(len(parts))]
    scratch = list(scratch)
    colbuf = [scratch.pop(0) for _ in range(PARTS_A)]
    rowbuf = [scratch.pop(0) for _ in parts]
    (own_tab, beta_tab, help_tab, alpha_signs, beta_signs, help_signs, shared,
     pairs_v, pairs_s, alpha_coef, beta_coef, help_coef, ssem, rsem, lsem) = scratch

    wide = width // PARTS_A
    spread = rows // cols
    blocks_b = blocks * spread
    tables = blocks * link_max
    chips = rows // 2
    reach = chips // 2
    across = chips // 2
    half = blocks // 2
    piece = tables // (2 * PIECES)
    helps = cols >= 4

    r = lax.axis_index("row")
    c = lax.axis_index("col")
    core = lax.rem(r, 2)
    chip = r // 2
    other = r + 1 - 2 * core
    place = jnp.where(chip < across, chip, chips - 1 - (chip - across))

    def chip_at(position):
        position = lax.rem(position + 2 * chips, chips)
        return jnp.where(position < across, position, across + (chips - 1 - position))

    def row_at(position, k):
        return 2 * chip_at(position) + k

    right = (row_at(place + 1, core), c)
    left = (row_at(place - 1, core), c)
    partner = (other, c)
    up = (r, jnp.minimum(c + 1, cols - 1))
    down = (r, jnp.maximum(c - 1, 0))
    has_up = c < cols - 1
    has_down = c > 0
    at_end = (c == 0) | (c == cols - 1)
    inner = jnp.logical_not(at_end)
    helper = (c == 1) | (c == cols - 2)
    aided = jnp.where(c == 1, 0, cols - 1)
    inward = (r, jnp.where(c == 0, 1, cols - 2))

    ids = {}

    def number(*key):
        return ids.setdefault(key, len(ids))

    pending = []

    def describe(src, dst, key, device):
        return pltpu.make_async_remote_copy(
            src_ref=src, dst_ref=dst, send_sem=ssem.at[number(*key)], recv_sem=rsem.at[number(*key)],
            device_id=device, device_id_type=MESH)

    def when(cond, action):
        if cond is None:
            action()
        else:
            pl.when(cond)(action)

    def send(src, dst, key, device, cond=None, drain=True):
        copy = describe(src, dst, key, device)
        if drain:
            pending.append((cond, copy))
        when(cond, copy.start)

    def arrive(ref, key, cond=None):
        when(cond, describe(ref, ref, key, partner).wait_recv)

    local = []

    def load(src, dst, cond=None):
        copy = pltpu.make_async_copy(src, dst, lsem.at[len(local)])
        local.append(copy)
        when(cond, copy.start)
        return lambda: when(cond, copy.wait)

    plan = []

    def at(time, action):
        plan.append((time, len(plan), action))

    barrier = pltpu.get_barrier_semaphore()
    for k in range(1, rows):
        pl.semaphore_signal(barrier, inc=1, device_id=(lax.rem(r + k, rows), c), device_id_type=MESH)

    @pl.when(has_up)
    def _():
        pl.semaphore_signal(barrier, inc=1, device_id=up, device_id_type=MESH)

    @pl.when(has_down)
    def _():
        pl.semaphore_signal(barrier, inc=1, device_id=down, device_id_type=MESH)

    wait_tab = load(tab, own_tab)
    wait_pairs = load(pairs, pairs_v.at[r])

    def load_rows(i):
        sem = lsem.at[len(local)]
        first = firsts[i]
        for k in range(blocks_b):
            pltpu.make_async_copy(
                v.at[first // size, pl.ds(first % size, parts[i][0]), pl.ds(k * size, size)],
                rowbuf[i].at[c * blocks_b + k], sem).start()
        ref = rowbuf[i].at[pl.ds(c * blocks_b, blocks_b)]
        local.append(pltpu.make_async_copy(ref, ref, sem))
        return local[-1].wait

    wait_rows = [load_rows(i) for i in range(len(parts))]
    wait_cols = [load(v.at[:, :, pl.ds(j * wide, wide)], colbuf[j].at[pl.ds(r * blocks, blocks)])
                 for j in range(PARTS_A)]

    pl.semaphore_wait(barrier, rows - 1 + has_up.astype(jnp.int32) + has_down.astype(jnp.int32))

    for k in range(1, rows):
        send(pairs, pairs_v.at[r], ("pairs", k), (lax.rem(r + k, rows), c))

    reach_up = {1: up, -1: down}

    def ends(k):
        return TILE * (chunks[k][3] + chunks[k][2]) / high

    def arrival(t, k, late):
        far = max(cols - 3, 1)
        tiles = max(1, min(t, far)) if late else min(t, far)
        return ends(k) + TILE * tiles + 3.0 * t + HOP * (t + 1)

    def row_chunk(k, tile):
        part, offset, count, _, _ = chunks[k]
        return rowbuf[part].at[pl.ds(tile * blocks_b, blocks_b), pl.ds(offset, count), :]

    def line_own(k, way, cond):
        helped = chunks[k][4]
        position = c if way == 1 else cols - 1 - c
        limit = cols - 2 if helped else cols - 1
        ref = row_chunk(k, c)
        send(ref, ref, ("line", way, k, 0), reach_up[way], cond & (position < limit))

    def line_arrive(k, way, t, edge):
        helped = chunks[k][4]
        last = cols - 2 if helped else cols - 1
        position = c if way == 1 else cols - 1 - c
        if edge:
            if t + 1 > last:
                return
            cond = position == t + 1
        else:
            if t + 2 > last:
                return
            cond = (position > t + 1) & (position <= last)
        ref = row_chunk(k, jnp.clip(c - way * (1 + t), 0, cols - 1))
        arrive(ref, ("line", way, k, t), cond)
        if edge:
            if t + 2 <= last:
                send(ref, ref, ("line", way, k, t + 1), reach_up[way], cond)
        elif t + 3 <= last:
            send(ref, ref, ("line", way, k, t + 1), reach_up[way], cond & (position < last))

    def table_places(s):
        source = c * spread + s
        source_chip = source // 2
        source_place = jnp.where(
            source_chip < across, source_chip, chips - 1 - (source_chip - across))
        distance = lax.rem(place - source_place + chips, chips)
        return lax.rem(source, 2), (distance, lax.rem(chips - distance, chips))

    ring = (right, left)

    def table_part(h, q):
        return pl.ds((h * PIECES + q) * piece, piece)

    def table_stage(s, h, q, d):
        source_core, hops = table_places(s)
        here = (core == source_core) & (hops[h] == d)
        part = table_part(h, q)
        ref = beta_tab.at[s, part]
        src = ref if d else tab.at[part]
        if d:
            arrive(ref, ("table", s, h, q), here)
        if d + 1 < chips:
            send(src, ref, ("table", s, h, q), ring[h], here, drain=False)
        send(src, ref, ("tableP", s, h, q), partner, here, drain=False)
        if helps:
            send(src, help_tab.at[s, part], ("help", s, h, q), inward, here & at_end, drain=False)

    def table_drain(s, h, q):
        source_core, hops = table_places(s)
        mine = core == source_core
        ref = beta_tab.at[s, table_part(h, q)]
        pending.append((mine & (hops[h] < chips - 1), describe(ref, ref, ("table", s, h, q), partner)))
        pending.append((mine, describe(ref, ref, ("tableP", s, h, q), partner)))
        if helps:
            pending.append((mine & at_end, describe(ref, ref, ("help", s, h, q), partner)))

    def table_finish():
        for s in range(spread):
            source_core, _ = table_places(s)
            for h in range(2):
                for q in range(PIECES):
                    arrive(beta_tab.at[s, table_part(h, q)], ("tableP", s, h, q), core != source_core)
            table_loads[s]()

    def help_arrive(s, h, q):
        source_core = table_places(s)[0]
        aided_core = lax.rem(aided * spread + s, 2)
        ref = help_tab.at[s, table_part(h, q)]
        arrive(ref, ("help", s, h, q), helper & (core == aided_core))
        send(ref, ref, ("helpP", s, h, q), partner, helper & (core == aided_core))

    def help_finish():
        for s in range(spread):
            aided_core = lax.rem(aided * spread + s, 2)
            for h in range(2):
                for q in range(PIECES):
                    arrive(help_tab.at[s, table_part(h, q)], ("helpP", s, h, q),
                           helper & (core != aided_core))

    def widen(source, base, target):
        @pl.loop(0, tables)
        def _(index):
            values = source[index].astype(jnp.float32).astype(jnp.bfloat16)
            target[base + index] = jnp.concatenate([values, values], axis=1)

    def widen_all(source, target):
        for s in range(spread):
            widen(source.at[s], s * tables, target)

    def tile_half(j, hb, position, k):
        return colbuf[j].at[pl.ds(row_at(position, k) * blocks + hb * half, half)]

    def ring_own(j, hb, way, cond, drain):
        ref = colbuf[j].at[pl.ds(r * blocks + hb * half, half)]
        src = v.at[pl.ds(hb * half, half), :, pl.ds(j * wide, wide)]
        send(src, ref, ("ring", way, j, hb, 0), ring[way], cond, drain=False)
        if drain:
            pending.append((None, describe(ref, ref, ("ring", way, j, hb, 0), partner)))

    def carried(way, hb, t):
        return t < reach - 1 or hb == way

    def ring_arrive(j, hb, way, t):
        ref = tile_half(j, hb, place - 1 - t if way == 0 else place + 1 + t, core)
        arrive(ref, ("ring", way, j, hb, t))
        if t + 1 < reach and carried(way, hb, t + 1):
            send(ref, ref, ("ring", way, j, hb, t + 1), ring[way])
        send(ref, ref, ("ringP", way, j, hb, t), partner)

    def ring_finish(j):
        wait_cols[j]()
        arrive(colbuf[j].at[pl.ds(other * blocks, blocks)], ("own", j))
        for t in range(reach):
            for way in range(2):
                for hb in range(2):
                    if carried(way, hb, t):
                        position = place - 1 - t if way == 0 else place + 1 + t
                        arrive(tile_half(j, hb, position, 1 - core), ("ringP", way, j, hb, t))

    def coefficients(target, first, count):
        @pl.loop(0, count)
        def _(b):
            block = first + b
            for l in range(link_max):
                pair = pairs_s[lax.div(block, blocks), lax.rem(block, blocks), l]
                norb = integrals.shape[0]
                value = integrals[lax.div(pair, norb), lax.rem(pair, norb)]
                target[b, l] = value * jnp.clip(counts[block] - l, 0, 1).astype(jnp.float32)

    def gather_pairs():
        wait_pairs()
        for k in range(1, rows):
            arrive(pairs_v.at[lax.rem(r - k + rows, rows)], ("pairs", k))
        copy = pltpu.make_async_copy(pairs_v, pairs_s, lsem.at[1])
        copy.start()
        copy.wait()
        coefficients(alpha_coef, r * blocks, blocks)
        coefficients(beta_coef, c * blocks_b, blocks_b)
        if helps:
            coefficients(help_coef, aided * blocks_b, blocks_b)

    def alpha_compute(j):
        @pl.loop(0, blocks)
        def _(block):
            total = jnp.zeros((size, wide), jnp.float32)
            for l in range(link_max):
                source = links[l, r * blocks + block]
                up_part, low_part = split(colbuf[j][source] * alpha_coef[block, l])
                total = total + jnp.dot(
                    alpha_signs[block * link_max + l], jnp.concatenate([up_part, low_part], axis=0),
                    preferred_element_type=jnp.float32)
            where = (pl.ds(pl.multiple_of(block * size, size), size), pl.ds(j * wide, wide))
            out[where] = out[where] + total

    def beta_compute(group, owner, coef, signs, target, start, add):
        count = sum(parts[i][0] for i in group)

        @pl.loop(0, blocks_b)
        def _(block):
            total = jnp.zeros((count, size), jnp.float32)
            for l in range(link_max):
                source = links[l, owner * blocks_b + block]
                value = jnp.concatenate([rowbuf[i][source] for i in group], axis=0)
                up_part, low_part = split(value * coef[block, l])
                total = total + lax.dot_general(
                    jnp.concatenate([up_part, low_part], axis=1), signs[block * link_max + l],
                    (((1,), (1,)), ((), ())), preferred_element_type=jnp.float32)
            where = (pl.ds(start, count), pl.ds(pl.multiple_of(block * size, size), size))
            if add:
                total = target[where] + total
            target[where] = total

    shared_first = sum(height for height, helped in parts if not helped)

    def own_beta(i, cond):
        def action():
            beta_compute([i], c, beta_coef, beta_signs, out, firsts[i], True)
        when(cond, action)

    def help_beta(i):
        @pl.when(helper)
        def _():
            beta_compute([i], aided, help_coef, help_signs, shared, firsts[i] - shared_first, False)

        ref = shared.at[pl.ds(firsts[i] - shared_first, parts[i][0])]
        send(ref, ref, ("sums", i), (r, aided), helper)

    def take_sums(i):
        ref = shared.at[pl.ds(firsts[i] - shared_first, parts[i][0])]
        arrive(ref, ("sums", i), at_end)

        @pl.when(at_end)
        def _():
            where = pl.ds(firsts[i], parts[i][0])
            out[where, :] = out[where, :] + ref[...]

    table_loads = []

    def begin():
        for s in range(spread):
            source_core, hops = table_places(s)
            table_loads.append(load(tab, beta_tab.at[s], (core == source_core) & (hops[0] == 0)))
        always = jnp.bool_(True)
        for k in range(len(chunks)):
            if chunks[k][1] == 0:
                wait_rows[chunks[k][0]]()
            early = always if k < EARLY or not helps else inner
            line_own(k, 1, early if k < EARLY or not helps else has_down)
            line_own(k, -1, early if k < EARLY or not helps else has_up)

    at(-2.0, begin)

    def rest():
        for k in range(EARLY, len(chunks)):
            line_own(k, 1, c == 0)
            line_own(k, -1, c == cols - 1)

    stage_last = PIECE * (PIECES - 1 + chips - 1) + HOP * (chips - 1)
    if helps:
        at(stage_last + 0.1, rest)

    for k in range(len(chunks)):
        for t in range(cols - 1):
            for edge in (False, True):
                late = edge and k >= EARLY and helps
                for way in (1, -1):
                    at(arrival(t, k, late), functools.partial(line_arrive, k, way, t, edge))

    for q in range(PIECES):
        for d in range(chips):
            for h in range(2):
                for s in range(spread):
                    time = -1.0 if d == 0 else PIECE * (q + d) + HOP * d
                    at(time, functools.partial(table_stage, s, h, q, d))
    at(stage_last + 3.5, table_finish)
    at(stage_last + 3.6, lambda: widen_all(beta_tab, beta_signs))

    if helps:
        helped_last = 0.0
        for q in range(PIECES):
            for h in range(2):
                time = 6.0 + max(TILE / 4 + PIECE * (2 * q + h + 1), PIECE * (q + chips) + HOP * (chips + 1))
                helped_last = max(helped_last, time)
                for s in range(spread):
                    at(time, functools.partial(help_arrive, s, h, q))
        at(helped_last + 1.5, help_finish)
        at(helped_last + 1.6, lambda: pl.when(helper)(lambda: widen_all(help_tab, help_signs)))

    order = []
    for j in range(PARTS_A):
        order.append((j, 0))
        if j:
            order.append((j - 1, 1))
    order.append((PARTS_A - 1, 1))
    step = TILE / (2 * PARTS_A)

    classes = []
    for h in range(2):
        kind = jnp.int32(chips - 1)
        for s in range(spread):
            source_core, hops = table_places(s)
            kind = jnp.where(core == source_core, hops[h], kind)
        classes.append(kind)

    begun = PIECE * PIECES
    for a, (j, second) in enumerate(order):
        for way in range(2):
            hb = (1 - way) if second else way
            for d in range(chips):
                if d == chips - 1:
                    time = max(0.0, 1.5 * step * a - 9.0)
                elif a < d:
                    time = 0.0
                else:
                    last = PIECE * (PIECES - 1 + d) + HOP * d if d else 0.0
                    time = max(last + 0.05, PIECE * (PIECES + d) + HOP * d + 1.5 * step * (a - d) - 9.0)
                at(time, functools.partial(ring_own, j, hb, way, classes[way] == d, d == 0))
            time = begun + 1.5 * step * a + step + HOP + 1.0
            for t in range(reach):
                if carried(way, hb, t):
                    at(time + 10.0 * t, functools.partial(ring_arrive, j, hb, way, t))

    def own_pass(j):
        ref = colbuf[j].at[pl.ds(r * blocks, blocks)]
        send(v.at[:, :, pl.ds(j * wide, wide)], ref, ("own", j), partner)

    for j in range(PARTS_A):
        at(0.5, functools.partial(own_pass, j))
        first = begun + 1.5 * step * order.index((j, 0)) + step + HOP + 1.0 + 10.0 * (reach - 1)
        second = begun + 1.5 * step * order.index((j, 1)) + step + HOP + 1.0 + 10.0 * max(reach - 2, 0)
        at(max(first, second) + 3.0, functools.partial(ring_finish, j))
        at(max(first, second) + 3.0, functools.partial(alpha_compute, j))

    def prepare():
        out[...] = jnp.zeros_like(out)
        gather_pairs()
        wait_tab()
        widen(own_tab, 0, alpha_signs)

    at(0.6, prepare)

    for i, (height, helped) in enumerate(parts):
        ks = [k for k, chunk in enumerate(chunks) if chunk[0] == i]
        late = helps and ks[-1] >= EARLY
        done = arrival(max(cols - 3, 0), ks[-1], late) + 0.1
        done_end = arrival(cols - 2, ks[-1], late) + 0.1
        if helped:
            at(done, functools.partial(help_beta, i))
            at(done, functools.partial(own_beta, i, inner))
            at(done_end + 12.0, functools.partial(take_sums, i))
        elif helps:
            at(done, functools.partial(own_beta, i, inner))
            at(done_end, functools.partial(own_beta, i, at_end))
        else:
            at(done_end, functools.partial(own_beta, i, None))

    for _, _, action in sorted(plan, key=lambda entry: entry[:2]):
        action()

    for s in range(spread):
        for h in range(2):
            for q in range(PIECES):
                table_drain(s, h, q)
    for cond, copy in pending:
        when(cond, copy.wait_send)


def local(vector, one_electron, links, counts, pairs, signs, rows, cols):
    blocks, link_max = pairs.shape
    size = signs.shape[2]
    high, width = vector.shape
    spread = rows // cols
    tables = blocks * link_max
    parts = row_parts(high, cols)
    helped = sum(height for height, aided in parts if aided)
    reach = rows // 4
    messages = rows - 1 + 2 * len(row_chunks(high, cols)) * (cols - 1)
    messages += PARTS_A * (1 + 8 * reach) + spread * 2 * PIECES * 4 + len(parts)
    scratch = [pltpu.VMEM((rows * blocks, size, width // PARTS_A), jnp.float32)] * PARTS_A
    scratch += [pltpu.VMEM((cols * blocks * spread, height, size), jnp.float32) for height, _ in parts]
    scratch += [
        pltpu.VMEM((tables, size, size), jnp.int32),
        pltpu.VMEM((spread, tables, size, size), jnp.int32),
        pltpu.VMEM((spread, tables, size, size), jnp.int32),
        pltpu.VMEM((tables, size, 2 * size), jnp.bfloat16),
        pltpu.VMEM((spread * tables, size, 2 * size), jnp.bfloat16),
        pltpu.VMEM((spread * tables, size, 2 * size), jnp.bfloat16),
        pltpu.VMEM((max(helped, 8), width), jnp.float32),
        pltpu.VMEM((rows, blocks, link_max), jnp.int32),
        pltpu.SMEM((rows, blocks, link_max), jnp.int32),
        pltpu.SMEM((blocks, link_max), jnp.float32),
        pltpu.SMEM((blocks * spread, link_max), jnp.float32),
        pltpu.SMEM((blocks * spread, link_max), jnp.float32),
        pltpu.SemaphoreType.DMA((messages,)),
        pltpu.SemaphoreType.DMA((messages,)),
        pltpu.SemaphoreType.DMA((2 + len(parts) + PARTS_A + spread,)),
    ]
    smem = pl.BlockSpec(memory_space=pltpu.SMEM)
    anywhere = pl.BlockSpec(memory_space=pl.ANY)
    return pl.pallas_call(
        functools.partial(kernel, rows, cols, blocks, link_max),
        out_shape=jax.ShapeDtypeStruct(vector.shape, jnp.float32),
        in_specs=[smem, smem, smem, anywhere, anywhere, anywhere],
        out_specs=pl.BlockSpec(memory_space=pltpu.VMEM),
        scratch_shapes=scratch,
        compiler_params=pltpu.CompilerParams(
            collective_id=0, has_side_effects=True, vmem_limit_bytes=60 << 20),
    )(links.T, counts, one_electron, pairs, vector.reshape(blocks, size, width),
      signs.reshape(tables, size, size))


def solution(mesh):
    in_specs = (P("row", "col"), P(), P(), P(), P("row", None), P("row", None, None, None))
    out_specs = P("row", "col")
    body = functools.partial(local, rows=mesh.shape["row"], cols=mesh.shape["col"])
    return jax.shard_map(body, mesh=mesh, in_specs=in_specs, out_specs=out_specs, check_vma=False)
```

time: 160 us -> 143 us (0.89)
  Pallas kernels: 150 us -> 140 us
  other arithmetic: 4.21 us -> 0 us
  local copies, waits for them, and re-layouts: 5.53 us -> 3.16 us
    pallas_call x1, Pallas kernels: 150 us -> 140 us  [local(): pl.pallas_call(functools.partial(kernel, rows, cols, blocks, link_max), o...]
    convert_element_type x1 -> x0, other arithmetic: 1.74 us -> none  [local(): signs.reshape(tables, size, size).astype(jnp.float32)]
    unnamed x4 -> x1, local copies, waits for them, and re-layouts: 3.85 us -> 3.16 us
where the time goes in v1:
time: 143 us
  Pallas kernels  140 us (98%)
  local copies, waits for them, and re-layouts  3.16 us (2%)
    pallas_call x1, Pallas kernels, local(): pl.pallas_call(functools.partial(kernel, rows, cols, blocks, link_max), o...  140 us
    unnamed x1, local copies, waits for them, and re-layouts  3.16 us

profile of v1, /device:TPU:0, one launch (start us, length us, event | category | flops | bytes accessed | tf_op | source)
XLA Modules:
  0.0 143.2 jit_solution(6122015697669551064)
XLA Ops:
  0.0 140.0 %shard_map.64 = f32[512,1024]{1,0:T(8,128)} custom-call(s32[8,32]{1,0:T(8,128)} %bitcast.5, s32[32]{0:T(128)} %counts.1, f32[16,16]{1,0:T(8,128)} %integrals.1, s32[4,8]{1,0:T(4,128)} %pairs.1, f32[4,128,1024]{2,1,0:T(8,128)} %bitcast.3, s32[32,128,128]{2,1,0:T(8,128)} %bitcast.4), custom_call_target="tpu_custom_call" | custom-call | tf_op jit(solution)/shard_map/pallas_call | solution.py:546
  140.0 3.2 %copy.8 = f32[512,1024]{1,0:T(8,128)} copy(f32[512,1024]{1,0:T(8,128)} %shard_map.64) | data formatting | bytes 4194304

commit v2 on v1

--- a/solution.py
+++ b/solution.py
@@ -10,7 +10,6 @@
 MESH = pl.DeviceIdType.MESH
 PARTS_A = 4
 PIECES = 4
-EARLY = 2
 TILE = 45.0
 HOP = 1.5
 PIECE = 5.6
@@ -24,21 +23,20 @@
 
 def row_parts(high, cols):
     helps = cols >= 4
-    quarter, eighth, last = high // 4, high // 8, high // 16
-    return [(quarter, False), (quarter, False), (quarter, helps), (eighth, helps), (last, helps), (last, helps)]
+    return [(high // 4, False)] + [(high // 8, helps)] * 5 + [(high // 16, helps)] * 2
 
 
 def row_chunks(high, cols):
     chunks, first = [], 0
     for part, (height, helped) in enumerate(row_parts(high, cols)):
-        piece = min(height, high // 8)
+        piece = min(height, high // 16 if part else high // 8)
         for offset in range(0, height, piece):
             chunks.append((part, offset, piece, first + offset, helped))
         first += height
     return chunks
 
 
-def kernel(rows, cols, blocks, link_max, links, counts, integrals, pairs, v, tab, out, *scratch):
+def kernel(rows, cols, blocks, link_max, links_in, counts_in, integrals_in, pairs, v, tab, out, *scratch):
     size = tab.shape[1]
     high, width = out.shape
     parts = row_parts(high, cols)
@@ -48,7 +46,8 @@
     colbuf = [scratch.pop(0) for _ in range(PARTS_A)]
     rowbuf = [scratch.pop(0) for _ in parts]
     (own_tab, beta_tab, help_tab, alpha_signs, beta_signs, help_signs, shared,
-     pairs_v, pairs_s, alpha_coef, beta_coef, help_coef, ssem, rsem, lsem) = scratch
+     pairs_v, pairs_s, links, counts, integrals, alpha_coef, beta_coef, help_coef,
+     ssem, rsem, lsem) = scratch
 
     wide = width // PARTS_A
     spread = rows // cols
@@ -60,6 +59,7 @@
     half = blocks // 2
     piece = tables // (2 * PIECES)
     helps = cols >= 4
+    early = [k for k, chunk in enumerate(chunks) if chunk[0] < 2]
 
     r = lax.axis_index("row")
     c = lax.axis_index("col")
@@ -140,8 +140,8 @@
     def _():
         pl.semaphore_signal(barrier, inc=1, device_id=down, device_id_type=MESH)
 
-    wait_tab = load(tab, own_tab)
-    wait_pairs = load(pairs, pairs_v.at[r])
+    wait_small = [load(pairs, pairs_v.at[r]), load(links_in, links), load(counts_in, counts),
+                  load(integrals_in, integrals)]
 
     def load_rows(i):
         sem = lsem.at[len(local)]
@@ -155,6 +155,7 @@
         return local[-1].wait
 
     wait_rows = [load_rows(i) for i in range(len(parts))]
+    wait_tab = load(tab, own_tab)
     wait_cols = [load(v.at[:, :, pl.ds(j * wide, wide)], colbuf[j].at[pl.ds(r * blocks, blocks)])
                  for j in range(PARTS_A)]
 
@@ -171,7 +172,8 @@
     def arrival(t, k, late):
         far = max(cols - 3, 1)
         tiles = max(1, min(t, far)) if late else min(t, far)
-        return ends(k) + TILE * tiles + 3.0 * t + HOP * (t + 1)
+        length = TILE * chunks[k][2] / high
+        return ends(k) + TILE * tiles + HOP + (length + HOP) * (t if late else max(t - far, 0))
 
     def row_chunk(k, tile):
         part, offset, count, _, _ = chunks[k]
@@ -184,25 +186,26 @@
         ref = row_chunk(k, c)
         send(ref, ref, ("line", way, k, 0), reach_up[way], cond & (position < limit))
 
-    def line_arrive(k, way, t, edge):
+    def line_arrive(k, way, t, edge, forward):
         helped = chunks[k][4]
         last = cols - 2 if helped else cols - 1
+        onward = t + 2 <= last if edge else t + 3 <= last
+        if onward != forward or (t + 1 > last if edge else t + 2 > last):
+            return
         position = c if way == 1 else cols - 1 - c
-        if edge:
-            if t + 1 > last:
-                return
-            cond = position == t + 1
-        else:
-            if t + 2 > last:
-                return
-            cond = (position > t + 1) & (position <= last)
+        cond = position == t + 1 if edge else (position > t + 1) & (position <= last)
         ref = row_chunk(k, jnp.clip(c - way * (1 + t), 0, cols - 1))
         arrive(ref, ("line", way, k, t), cond)
-        if edge:
-            if t + 2 <= last:
-                send(ref, ref, ("line", way, k, t + 1), reach_up[way], cond)
-        elif t + 3 <= last:
-            send(ref, ref, ("line", way, k, t + 1), reach_up[way], cond & (position < last))
+        if onward:
+            send(ref, ref, ("line", way, k, t + 1), reach_up[way], cond if edge else cond & (position < last))
+
+    def line_finish(i):
+        for k, chunk in enumerate(chunks):
+            if chunk[0] == i:
+                for way in (1, -1):
+                    for t in range(cols - 1):
+                        for edge in (False, True):
+                            line_arrive(k, way, t, edge, False)
 
     def table_places(s):
         source = c * spread + s
@@ -263,15 +266,24 @@
                     arrive(help_tab.at[s, table_part(h, q)], ("helpP", s, h, q),
                            helper & (core != aided_core))
 
+    def narrow(value):
+        return value.astype(jnp.float32).astype(jnp.bfloat16)
+
     def widen(source, base, target):
         @pl.loop(0, tables)
         def _(index):
-            values = source[index].astype(jnp.float32).astype(jnp.bfloat16)
+            values = narrow(source[index])
             target[base + index] = jnp.concatenate([values, values], axis=1)
 
-    def widen_all(source, target):
+    def couple(source, base, target):
+        @pl.loop(0, tables // 2)
+        def _(index):
+            target[base + index] = jnp.concatenate(
+                [narrow(source[2 * index]), narrow(source[2 * index + 1])], axis=1)
+
+    def couple_all(source, target):
         for s in range(spread):
-            widen(source.at[s], s * tables, target)
+            couple(source.at[s], s * (tables // 2), target)
 
     def tile_half(j, hb, position, k):
         return colbuf[j].at[pl.ds(row_at(position, k) * blocks + hb * half, half)]
@@ -314,10 +326,11 @@
                 target[b, l] = value * jnp.clip(counts[block] - l, 0, 1).astype(jnp.float32)
 
     def gather_pairs():
-        wait_pairs()
+        for wait in wait_small:
+            wait()
         for k in range(1, rows):
             arrive(pairs_v.at[lax.rem(r - k + rows, rows)], ("pairs", k))
-        copy = pltpu.make_async_copy(pairs_v, pairs_s, lsem.at[1])
+        copy = pltpu.make_async_copy(pairs_v, pairs_s, lsem.at[0])
         copy.start()
         copy.wait()
         coefficients(alpha_coef, r * blocks, blocks)
@@ -343,14 +356,21 @@
 
         @pl.loop(0, blocks_b)
         def _(block):
-            total = jnp.zeros((count, size), jnp.float32)
-            for l in range(link_max):
-                source = links[l, owner * blocks_b + block]
-                value = jnp.concatenate([rowbuf[i][source] for i in group], axis=0)
-                up_part, low_part = split(value * coef[block, l])
+            total = jnp.zeros((2 * count, size), jnp.float32)
+            for l in range(0, link_max, 2):
+                highs, lows = [], []
+                for m in (l, l + 1):
+                    source = links[m, owner * blocks_b + block]
+                    value = jnp.concatenate([rowbuf[i][source] for i in group], axis=0)
+                    up_part, low_part = split(value * coef[block, m])
+                    highs.append(up_part)
+                    lows.append(low_part)
+                value = jnp.concatenate(
+                    [jnp.concatenate(highs, axis=1), jnp.concatenate(lows, axis=1)], axis=0)
                 total = total + lax.dot_general(
-                    jnp.concatenate([up_part, low_part], axis=1), signs[block * link_max + l],
+                    value, signs[block * (link_max // 2) + l // 2],
                     (((1,), (1,)), ((), ())), preferred_element_type=jnp.float32)
+            total = total[:count] + total[count:]
             where = (pl.ds(start, count), pl.ds(pl.multiple_of(block * size, size), size))
             if add:
                 total = target[where] + total
@@ -358,9 +378,9 @@
 
     shared_first = sum(height for height, helped in parts if not helped)
 
-    def own_beta(i, cond):
+    def own_beta(group, cond):
         def action():
-            beta_compute([i], c, beta_coef, beta_signs, out, firsts[i], True)
+            beta_compute(group, c, beta_coef, beta_signs, out, firsts[group[0]], True)
         when(cond, action)
 
     def help_beta(i):
@@ -390,14 +410,14 @@
         for k in range(len(chunks)):
             if chunks[k][1] == 0:
                 wait_rows[chunks[k][0]]()
-            early = always if k < EARLY or not helps else inner
-            line_own(k, 1, early if k < EARLY or not helps else has_down)
-            line_own(k, -1, early if k < EARLY or not helps else has_up)
+            first = k in early or not helps
+            line_own(k, 1, always if first else has_down)
+            line_own(k, -1, always if first else has_up)
 
     at(-2.0, begin)
 
     def rest():
-        for k in range(EARLY, len(chunks)):
+        for k in range(len(early), len(chunks)):
             line_own(k, 1, c == 0)
             line_own(k, -1, c == cols - 1)
 
@@ -408,9 +428,9 @@
     for k in range(len(chunks)):
         for t in range(cols - 1):
             for edge in (False, True):
-                late = edge and k >= EARLY and helps
+                late = edge and k not in early and helps
                 for way in (1, -1):
-                    at(arrival(t, k, late), functools.partial(line_arrive, k, way, t, edge))
+                    at(arrival(t, k, late), functools.partial(line_arrive, k, way, t, edge, True))
 
     for q in range(PIECES):
         for d in range(chips):
@@ -419,8 +439,9 @@
                     time = -1.0 if d == 0 else PIECE * (q + d) + HOP * d
                     at(time, functools.partial(table_stage, s, h, q, d))
     at(stage_last + 3.5, table_finish)
-    at(stage_last + 3.6, lambda: widen_all(beta_tab, beta_signs))
-
+    at(stage_last + 3.6, lambda: couple_all(beta_tab, beta_signs))
+
+    help_ready = 0.0
     if helps:
         helped_last = 0.0
         for q in range(PIECES):
@@ -430,14 +451,10 @@
                 for s in range(spread):
                     at(time, functools.partial(help_arrive, s, h, q))
         at(helped_last + 1.5, help_finish)
-        at(helped_last + 1.6, lambda: pl.when(helper)(lambda: widen_all(help_tab, help_signs)))
-
-    order = []
-    for j in range(PARTS_A):
-        order.append((j, 0))
-        if j:
-            order.append((j - 1, 1))
-    order.append((PARTS_A - 1, 1))
+        at(helped_last + 1.6, lambda: pl.when(helper)(lambda: couple_all(help_tab, help_signs)))
+        help_ready = helped_last + 1.7
+
+    order = [(j, second) for second in range(2) for j in range(PARTS_A)]
     step = TILE / (2 * PARTS_A)
 
     classes = []
@@ -449,22 +466,24 @@
         classes.append(kind)
 
     begun = PIECE * PIECES
+
+    def ring_time(a, t):
+        if t == 0:
+            wait = PIECE * (PIECES + max(chips - 2, 0)) + HOP * chips + step * (a - 1)
+            return wait if a else begun + step + HOP
+        return begun + TILE + step * (a % PARTS_A + 1) + HOP + 1.0 + 30.0 * (t - 1) + 0.1 * (a // PARTS_A)
+
     for a, (j, second) in enumerate(order):
         for way in range(2):
             hb = (1 - way) if second else way
             for d in range(chips):
-                if d == chips - 1:
-                    time = max(0.0, 1.5 * step * a - 9.0)
-                elif a < d:
-                    time = 0.0
-                else:
-                    last = PIECE * (PIECES - 1 + d) + HOP * d if d else 0.0
-                    time = max(last + 0.05, PIECE * (PIECES + d) + HOP * d + 1.5 * step * (a - d) - 9.0)
+                time = 0.0
+                if d < chips - 1 and a >= d:
+                    time = PIECE * (PIECES - 1 + d) + HOP * d + 0.05 if d else 0.0
                 at(time, functools.partial(ring_own, j, hb, way, classes[way] == d, d == 0))
-            time = begun + 1.5 * step * a + step + HOP + 1.0
             for t in range(reach):
                 if carried(way, hb, t):
-                    at(time + 10.0 * t, functools.partial(ring_arrive, j, hb, way, t))
+                    at(ring_time(a, t), functools.partial(ring_arrive, j, hb, way, t))
 
     def own_pass(j):
         ref = colbuf[j].at[pl.ds(r * blocks, blocks)]
@@ -472,10 +491,9 @@
 
     for j in range(PARTS_A):
         at(0.5, functools.partial(own_pass, j))
-        first = begun + 1.5 * step * order.index((j, 0)) + step + HOP + 1.0 + 10.0 * (reach - 1)
-        second = begun + 1.5 * step * order.index((j, 1)) + step + HOP + 1.0 + 10.0 * max(reach - 2, 0)
-        at(max(first, second) + 3.0, functools.partial(ring_finish, j))
-        at(max(first, second) + 3.0, functools.partial(alpha_compute, j))
+        done = max(ring_time(j, reach - 1), ring_time(PARTS_A + j, max(reach - 2, 0))) + 2.5
+        at(done, functools.partial(ring_finish, j))
+        at(done, functools.partial(alpha_compute, j))
 
     def prepare():
         out[...] = jnp.zeros_like(out)
@@ -485,20 +503,27 @@
 
     at(0.6, prepare)
 
+    groups = [[0], [1, 2], [3, 4], [5, 6, 7]]
+
+    def finish_time(i, t):
+        k = max(k for k, chunk in enumerate(chunks) if chunk[0] == i)
+        return arrival(t, k, helps and k not in early) + 0.1
+
     for i, (height, helped) in enumerate(parts):
-        ks = [k for k, chunk in enumerate(chunks) if chunk[0] == i]
-        late = helps and ks[-1] >= EARLY
-        done = arrival(max(cols - 3, 0), ks[-1], late) + 0.1
-        done_end = arrival(cols - 2, ks[-1], late) + 0.1
+        inside, outside = finish_time(i, max(cols - 3, 0)), finish_time(i, cols - 2)
         if helped:
-            at(done, functools.partial(help_beta, i))
-            at(done, functools.partial(own_beta, i, inner))
-            at(done_end + 12.0, functools.partial(take_sums, i))
-        elif helps:
-            at(done, functools.partial(own_beta, i, inner))
-            at(done_end, functools.partial(own_beta, i, at_end))
+            inside = max(inside, help_ready) if i == 1 else inside
+            at(inside, functools.partial(line_finish, i))
+            at(inside, functools.partial(help_beta, i))
+            at(outside + 15.0 + i, functools.partial(take_sums, i))
         else:
-            at(done_end, functools.partial(own_beta, i, None))
+            at(outside, functools.partial(line_finish, i))
+    for group in groups:
+        inside, outside = finish_time(group[-1], max(cols - 3, 0)), finish_time(group[-1], cols - 2)
+        if parts[group[0]][1]:
+            at(max(inside, help_ready) + 0.1, functools.partial(own_beta, group, inner))
+        else:
+            at(outside + 0.1, functools.partial(own_beta, group, None))
 
     for _, _, action in sorted(plan, key=lambda entry: entry[:2]):
         action()
@@ -529,30 +554,33 @@
         pltpu.VMEM((spread, tables, size, size), jnp.int32),
         pltpu.VMEM((spread, tables, size, size), jnp.int32),
         pltpu.VMEM((tables, size, 2 * size), jnp.bfloat16),
-        pltpu.VMEM((spread * tables, size, 2 * size), jnp.bfloat16),
-        pltpu.VMEM((spread * tables, size, 2 * size), jnp.bfloat16),
+        pltpu.VMEM((spread * tables // 2, size, 2 * size), jnp.bfloat16),
+        pltpu.VMEM((spread * tables // 2, size, 2 * size), jnp.bfloat16),
         pltpu.VMEM((max(helped, 8), width), jnp.float32),
         pltpu.VMEM((rows, blocks, link_max), jnp.int32),
         pltpu.SMEM((rows, blocks, link_max), jnp.int32),
+        pltpu.SMEM((link_max, links.shape[0]), jnp.int32),
+        pltpu.SMEM(counts.shape, jnp.int32),
+        pltpu.SMEM(one_electron.shape, jnp.float32),
         pltpu.SMEM((blocks, link_max), jnp.float32),
         pltpu.SMEM((blocks * spread, link_max), jnp.float32),
         pltpu.SMEM((blocks * spread, link_max), jnp.float32),
         pltpu.SemaphoreType.DMA((messages,)),
         pltpu.SemaphoreType.DMA((messages,)),
-        pltpu.SemaphoreType.DMA((2 + len(parts) + PARTS_A + spread,)),
+        pltpu.SemaphoreType.DMA((5 + len(parts) + PARTS_A + spread,)),
     ]
-    smem = pl.BlockSpec(memory_space=pltpu.SMEM)
-    anywhere = pl.BlockSpec(memory_space=pl.ANY)
+    far = pl.BlockSpec(memory_space=pltpu.HBM)
+    operands = (links.T, counts, one_electron, pairs, vector.reshape(blocks, size, width),
+                signs.reshape(tables, size, size))
     return pl.pallas_call(
         functools.partial(kernel, rows, cols, blocks, link_max),
         out_shape=jax.ShapeDtypeStruct(vector.shape, jnp.float32),
-        in_specs=[smem, smem, smem, anywhere, anywhere, anywhere],
+        in_specs=[far] * 6,
         out_specs=pl.BlockSpec(memory_space=pltpu.VMEM),
         scratch_shapes=scratch,
         compiler_params=pltpu.CompilerParams(
-            collective_id=0, has_side_effects=True, vmem_limit_bytes=60 << 20),
-    )(links.T, counts, one_electron, pairs, vector.reshape(blocks, size, width),
-      signs.reshape(tables, size, size))
+            collective_id=0, has_side_effects=True, vmem_limit_bytes=48 << 20),
+    )(*[pltpu.with_memory_space_constraint(value, pltpu.HBM) for value in operands])
 
 
 def solution(mesh):

time: 143 us -> 129 us (0.902)
  Pallas kernels: 140 us -> 127 us
  local copies, waits for them, and re-layouts: 3.16 us -> 1.32 us
    pallas_call x1, Pallas kernels: 140 us -> 127 us  [local(): pl.pallas_call(functools.partial(kernel, rows, cols, blocks, link_max), o...]
    unnamed x1, local copies, waits for them, and re-layouts: 3.16 us -> 1.32 us
where the time goes in v2:
time: 129 us
  Pallas kernels  127 us (98%)
  local copies, waits for them, and re-layouts  1.32 us (1%)
    pallas_call x1, Pallas kernels, local(): pl.pallas_call(functools.partial(kernel, rows, cols, blocks, link_max), o...  127 us

profile of v2, /device:TPU:0, one launch (start us, length us, event | category | flops | bytes accessed | tf_op | source)
XLA Modules:
  0.0 128.6 jit_solution(17603747418820652088)
XLA Ops:
  0.0 127.3 %shard_map.64 = f32[512,1024]{1,0:T(8,128)S(1)} custom-call(s32[8,32]{1,0:T(8,128)} %bitcast.5, s32[32]{0:T(128)} %counts_in.1, f32[16,16]{1,0:T(8,128)} %integrals_in.1, s32[4,8]{1,0:T(4,128)} %pairs.1, f32[4,128,1024]{2,1,0:T(8,128)} %bitcast.3, s32[32,128,128]{2,1,0:T(8,128)} %bitcast.4), custom_call_target="tpu_custom_call" | custom-call | tf_op jit(solution)/shard_map/pallas_call | solution.py:575
  127.3 1.3 %copy.8 = f32[512,1024]{1,0:T(8,128)} copy(f32[512,1024]{1,0:T(8,128)S(1)} %shard_map.64) | data formatting | bytes 4194304

commit v3 on v2

--- a/solution.py
+++ b/solution.py
@@ -10,6 +10,7 @@
 MESH = pl.DeviceIdType.MESH
 PARTS_A = 4
 PIECES = 4
+START = 4.5
 TILE = 45.0
 HOP = 1.5
 PIECE = 5.6
@@ -36,9 +37,22 @@
     return chunks
 
 
-def kernel(rows, cols, blocks, link_max, links_in, counts_in, integrals_in, pairs, v, tab, out, *scratch):
+def in_order(plan):
+    left = sorted(enumerate(plan), key=lambda entry: (entry[1][0], entry[0]))
+    now, result = 0.0, []
+    while left:
+        ready = [entry for entry in left if entry[1][0] <= now] or [left[0]]
+        chosen = min(ready, key=lambda entry: (entry[1][1], entry[1][0], entry[0]))
+        left.remove(chosen)
+        start, _, length, action = chosen[1]
+        now = max(now, start) + length
+        result.append(action)
+    return result
+
+
+def kernel(rows, cols, blocks, link_max, links_in, counts_in, integrals_in, pairs, v, tab, result, *scratch):
     size = tab.shape[1]
-    high, width = out.shape
+    high, width = result.shape
     parts = row_parts(high, cols)
     chunks = row_chunks(high, cols)
     firsts = [sum(p[0] for p in parts[:i]) for i in range(len(parts))]
@@ -46,7 +60,7 @@
     colbuf = [scratch.pop(0) for _ in range(PARTS_A)]
     rowbuf = [scratch.pop(0) for _ in parts]
     (own_tab, beta_tab, help_tab, alpha_signs, beta_signs, help_signs, shared,
-     pairs_v, pairs_s, links, counts, integrals, alpha_coef, beta_coef, help_coef,
+     out, pairs_v, pairs_s, links, counts, integrals, alpha_coef, beta_coef, help_coef,
      ssem, rsem, lsem) = scratch
 
     wide = width // PARTS_A
@@ -88,16 +102,19 @@
     aided = jnp.where(c == 1, 0, cols - 1)
     inward = (r, jnp.where(c == 0, 1, cols - 2))
 
-    ids = {}
-
-    def number(*key):
-        return ids.setdefault(key, len(ids))
-
-    pending = []
-
-    def describe(src, dst, key, device):
+    numbers = ({}, {})
+
+    def number(side, key):
+        return numbers[side].setdefault(key, len(numbers[side]))
+
+    plan = []
+
+    def at(time, action, rank=0, length=0.0):
+        plan.append((time, rank, length, action))
+
+    def describe(src, dst, group, key, device):
         return pltpu.make_async_remote_copy(
-            src_ref=src, dst_ref=dst, send_sem=ssem.at[number(*key)], recv_sem=rsem.at[number(*key)],
+            src_ref=src, dst_ref=dst, send_sem=ssem.at[number(0, group)], recv_sem=rsem.at[number(1, key)],
             device_id=device, device_id_type=MESH)
 
     def when(cond, action):
@@ -106,14 +123,17 @@
         else:
             pl.when(cond)(action)
 
-    def send(src, dst, key, device, cond=None, drain=True):
-        copy = describe(src, dst, key, device)
-        if drain:
-            pending.append((cond, copy))
-        when(cond, copy.start)
+    def send(src, dst, group, key, device, cond=None):
+        when(cond, describe(src, dst, group, key, device).start)
 
     def arrive(ref, key, cond=None):
-        when(cond, describe(ref, ref, key, partner).wait_recv)
+        when(cond, pltpu.make_async_copy(ref, ref, rsem.at[number(1, key)]).wait)
+
+    def drain(time, ref, group, cond=None):
+        def action():
+            wait = pltpu.make_async_copy(ref, ref, ssem.at[number(0, group)]).wait
+            when(cond() if cond else None, wait)
+        at(time, action, 9, 0.02)
 
     local = []
 
@@ -122,11 +142,6 @@
         local.append(copy)
         when(cond, copy.start)
         return lambda: when(cond, copy.wait)
-
-    plan = []
-
-    def at(time, action):
-        plan.append((time, len(plan), action))
 
     barrier = pltpu.get_barrier_semaphore()
     for k in range(1, rows):
@@ -162,7 +177,8 @@
     pl.semaphore_wait(barrier, rows - 1 + has_up.astype(jnp.int32) + has_down.astype(jnp.int32))
 
     for k in range(1, rows):
-        send(pairs, pairs_v.at[r], ("pairs", k), (lax.rem(r + k, rows), c))
+        send(pairs, pairs_v.at[r], ("pairs", k), ("pairs", k), (lax.rem(r + k, rows), c))
+        drain(15.0, pairs_v.at[r], ("pairs", k))
 
     reach_up = {1: up, -1: down}
 
@@ -184,7 +200,7 @@
         position = c if way == 1 else cols - 1 - c
         limit = cols - 2 if helped else cols - 1
         ref = row_chunk(k, c)
-        send(ref, ref, ("line", way, k, 0), reach_up[way], cond & (position < limit))
+        send(ref, ref, ("line", way, 0, helped), ("line", way, k, 0), reach_up[way], cond & (position < limit))
 
     def line_arrive(k, way, t, edge, forward):
         helped = chunks[k][4]
@@ -197,7 +213,8 @@
         ref = row_chunk(k, jnp.clip(c - way * (1 + t), 0, cols - 1))
         arrive(ref, ("line", way, k, t), cond)
         if onward:
-            send(ref, ref, ("line", way, k, t + 1), reach_up[way], cond if edge else cond & (position < last))
+            send(ref, ref, ("line", way, t + 1, helped), ("line", way, k, t + 1), reach_up[way],
+                 cond if edge else cond & (position < last))
 
     def line_finish(i):
         for k, chunk in enumerate(chunks):
@@ -225,30 +242,19 @@
         here = (core == source_core) & (hops[h] == d)
         part = table_part(h, q)
         ref = beta_tab.at[s, part]
-        src = ref if d else tab.at[part]
+        src = ref if d else own_tab.at[part]
         if d:
             arrive(ref, ("table", s, h, q), here)
         if d + 1 < chips:
-            send(src, ref, ("table", s, h, q), ring[h], here, drain=False)
-        send(src, ref, ("tableP", s, h, q), partner, here, drain=False)
+            send(src, ref, ("table", s, h), ("table", s, h, q), ring[h], here)
+        send(src, ref, ("tableP", s), ("tableP", s), partner, here)
         if helps:
-            send(src, help_tab.at[s, part], ("help", s, h, q), inward, here & at_end, drain=False)
-
-    def table_drain(s, h, q):
-        source_core, hops = table_places(s)
-        mine = core == source_core
-        ref = beta_tab.at[s, table_part(h, q)]
-        pending.append((mine & (hops[h] < chips - 1), describe(ref, ref, ("table", s, h, q), partner)))
-        pending.append((mine, describe(ref, ref, ("tableP", s, h, q), partner)))
-        if helps:
-            pending.append((mine & at_end, describe(ref, ref, ("help", s, h, q), partner)))
+            send(src, help_tab.at[s, part], ("help", s), ("help", s, h, q), inward, here & at_end)
 
     def table_finish():
         for s in range(spread):
             source_core, _ = table_places(s)
-            for h in range(2):
-                for q in range(PIECES):
-                    arrive(beta_tab.at[s, table_part(h, q)], ("tableP", s, h, q), core != source_core)
+            arrive(beta_tab.at[s], ("tableP", s), core != source_core)
             table_loads[s]()
 
     def help_arrive(s, h, q):
@@ -256,15 +262,12 @@
         aided_core = lax.rem(aided * spread + s, 2)
         ref = help_tab.at[s, table_part(h, q)]
         arrive(ref, ("help", s, h, q), helper & (core == aided_core))
-        send(ref, ref, ("helpP", s, h, q), partner, helper & (core == aided_core))
+        send(ref, ref, ("helpP", s), ("helpP", s), partner, helper & (core == aided_core))
 
     def help_finish():
         for s in range(spread):
             aided_core = lax.rem(aided * spread + s, 2)
-            for h in range(2):
-                for q in range(PIECES):
-                    arrive(help_tab.at[s, table_part(h, q)], ("helpP", s, h, q),
-                           helper & (core != aided_core))
+            arrive(help_tab.at[s], ("helpP", s), helper & (core != aided_core))
 
     def narrow(value):
         return value.astype(jnp.float32).astype(jnp.bfloat16)
@@ -288,12 +291,9 @@
     def tile_half(j, hb, position, k):
         return colbuf[j].at[pl.ds(row_at(position, k) * blocks + hb * half, half)]
 
-    def ring_own(j, hb, way, cond, drain):
+    def ring_own(j, hb, way, cond):
         ref = colbuf[j].at[pl.ds(r * blocks + hb * half, half)]
-        src = v.at[pl.ds(hb * half, half), :, pl.ds(j * wide, wide)]
-        send(src, ref, ("ring", way, j, hb, 0), ring[way], cond, drain=False)
-        if drain:
-            pending.append((None, describe(ref, ref, ("ring", way, j, hb, 0), partner)))
+        send(ref, ref, ("ring", way, 0), ("ring", way, j, hb, 0), ring[way], cond)
 
     def carried(way, hb, t):
         return t < reach - 1 or hb == way
@@ -302,18 +302,11 @@
         ref = tile_half(j, hb, place - 1 - t if way == 0 else place + 1 + t, core)
         arrive(ref, ("ring", way, j, hb, t))
         if t + 1 < reach and carried(way, hb, t + 1):
-            send(ref, ref, ("ring", way, j, hb, t + 1), ring[way])
-        send(ref, ref, ("ringP", way, j, hb, t), partner)
+            send(ref, ref, ("ring", way, t + 1), ("ring", way, j, hb, t + 1), ring[way])
+        send(ref, ref, ("ringP", way, t), ("tiles", j), partner)
 
     def ring_finish(j):
-        wait_cols[j]()
-        arrive(colbuf[j].at[pl.ds(other * blocks, blocks)], ("own", j))
-        for t in range(reach):
-            for way in range(2):
-                for hb in range(2):
-                    if carried(way, hb, t):
-                        position = place - 1 - t if way == 0 else place + 1 + t
-                        arrive(tile_half(j, hb, position, 1 - core), ("ringP", way, j, hb, t))
+        arrive(colbuf[j].at[pl.ds(0, chips * blocks)], ("tiles", j))
 
     def coefficients(target, first, count):
         @pl.loop(0, count)
@@ -389,7 +382,7 @@
             beta_compute([i], aided, help_coef, help_signs, shared, firsts[i] - shared_first, False)
 
         ref = shared.at[pl.ds(firsts[i] - shared_first, parts[i][0])]
-        send(ref, ref, ("sums", i), (r, aided), helper)
+        send(ref, ref, ("sums",), ("sums", i), (r, aided), helper)
 
     def take_sums(i):
         ref = shared.at[pl.ds(firsts[i] - shared_first, parts[i][0])]
@@ -400,12 +393,20 @@
             where = pl.ds(firsts[i], parts[i][0])
             out[where, :] = out[where, :] + ref[...]
 
+        flush(firsts[i], parts[i][0], at_end)
+
+    flushes, held, alphas = [], [], []
+
+    def flush(first, count, cond):
+        if len(alphas) < PARTS_A:
+            held.append((first, count, cond))
+            return
+        where = pl.ds(first, count)
+        flushes.append(load(out.at[where], result.at[where], cond))
+
     table_loads = []
 
     def begin():
-        for s in range(spread):
-            source_core, hops = table_places(s)
-            table_loads.append(load(tab, beta_tab.at[s], (core == source_core) & (hops[0] == 0)))
         always = jnp.bool_(True)
         for k in range(len(chunks)):
             if chunks[k][1] == 0:
@@ -413,46 +414,85 @@
             first = k in early or not helps
             line_own(k, 1, always if first else has_down)
             line_own(k, -1, always if first else has_up)
-
-    at(-2.0, begin)
+        wait_tab()
+
+    def begin_tables():
+        for s in range(spread):
+            source_core, hops = table_places(s)
+            table_loads.append(load(tab, beta_tab.at[s], (core == source_core) & (hops[0] == 0)))
+
+    def begin_tiles():
+        for j in range(PARTS_A):
+            wait_cols[j]()
+
+    at(-4.0, begin)
+    at(-2.0, begin_tables)
+    at(-1.5, begin_tiles)
 
     def rest():
         for k in range(len(early), len(chunks)):
             line_own(k, 1, c == 0)
             line_own(k, -1, c == cols - 1)
 
-    stage_last = PIECE * (PIECES - 1 + chips - 1) + HOP * (chips - 1)
+    stage_last = START + PIECE * (PIECES - 1 + chips - 1) + HOP * (chips - 1)
     if helps:
         at(stage_last + 0.1, rest)
 
     for k in range(len(chunks)):
-        for t in range(cols - 1):
-            for edge in (False, True):
-                late = edge and k not in early and helps
-                for way in (1, -1):
-                    at(arrival(t, k, late), functools.partial(line_arrive, k, way, t, edge, True))
+        helped = chunks[k][4]
+        late_k = helps and k not in early
+        for way in (1, -1):
+            for t in range(cols - 1):
+                for edge in (False, True):
+                    late = edge and late_k
+                    at(START + arrival(t, k, late), functools.partial(line_arrive, k, way, t, edge, True))
+
+    for helped in (False, True) if helps else (False,):
+        count = sum(height for height, aided_part in parts if aided_part == helped)
+        last_k = max(k for k, chunk in enumerate(chunks) if chunk[4] == helped)
+        last = cols - 2 if helped else cols - 1
+        for way in (1, -1):
+            for t in range(last):
+                def cond(t=t, way=way, last=last):
+                    position = c if way == 1 else cols - 1 - c
+                    return (position >= t) & (position < last)
+
+                sent = START + arrival(t, last_k, helps and last_k not in early) + (TILE if t == 0 else 0.0)
+                drain(sent + 6.0, out.at[pl.ds(0, count)], ("line", way, t, helped), cond)
 
     for q in range(PIECES):
-        for d in range(chips):
-            for h in range(2):
-                for s in range(spread):
-                    time = -1.0 if d == 0 else PIECE * (q + d) + HOP * d
+        for h in range(2):
+            for s in range(spread):
+                for d in range(chips):
+                    time = -1.0 if d == 0 else START + PIECE * (q + d) + HOP * d
                     at(time, functools.partial(table_stage, s, h, q, d))
-    at(stage_last + 3.5, table_finish)
-    at(stage_last + 3.6, lambda: couple_all(beta_tab, beta_signs))
+    for s in range(spread):
+        def mine(s=s):
+            return core == table_places(s)[0]
+
+        for h in range(2):
+            drain(stage_last + 12.0, beta_tab.at[s, pl.ds(0, tables // 2)], ("table", s, h),
+                  lambda s=s, h=h: mine(s) & (table_places(s)[1][h] < chips - 1))
+        drain(stage_last + 12.0, beta_tab.at[s], ("tableP", s), mine)
+        if helps:
+            drain(START + 1.8 * TILE, beta_tab.at[s], ("help", s), lambda s=s: mine(s) & at_end)
+            drain(START + 1.8 * TILE, beta_tab.at[s], ("helpP", s),
+                  lambda s=s: helper & (core == lax.rem(aided * spread + s, 2)))
+    at(stage_last + 4.0, table_finish, 1, 0.1)
+    at(stage_last + 4.1, lambda: couple_all(beta_tab, beta_signs), 2, 1.0)
 
     help_ready = 0.0
     if helps:
-        helped_last = 0.0
         for q in range(PIECES):
             for h in range(2):
-                time = 6.0 + max(TILE / 4 + PIECE * (2 * q + h + 1), PIECE * (q + chips) + HOP * (chips + 1))
-                helped_last = max(helped_last, time)
+                time = START + max(
+                    ends(len(early) - 1) + PIECE * (q + PIECES + 1) + HOP, PIECE * (q + chips) + HOP * (chips + 1))
+                help_ready = max(help_ready, time + 1.5)
                 for s in range(spread):
-                    at(time, functools.partial(help_arrive, s, h, q))
-        at(helped_last + 1.5, help_finish)
-        at(helped_last + 1.6, lambda: pl.when(helper)(lambda: couple_all(help_tab, help_signs)))
-        help_ready = helped_last + 1.7
+                    at(time + 0.5, functools.partial(help_arrive, s, h, q))
+        at(help_ready, help_finish, 1, 0.1)
+        at(help_ready + 0.1, lambda: pl.when(helper)(lambda: couple_all(help_tab, help_signs)), 1, 1.0)
+        help_ready += 0.2
 
     order = [(j, second) for second in range(2) for j in range(PARTS_A)]
     step = TILE / (2 * PARTS_A)
@@ -465,13 +505,15 @@
             kind = jnp.where(core == source_core, hops[h], kind)
         classes.append(kind)
 
-    begun = PIECE * PIECES
+    held_back = PARTS_A + 1
 
     def ring_time(a, t):
-        if t == 0:
-            wait = PIECE * (PIECES + max(chips - 2, 0)) + HOP * chips + step * (a - 1)
-            return wait if a else begun + step + HOP
-        return begun + TILE + step * (a % PARTS_A + 1) + HOP + 1.0 + 30.0 * (t - 1) + 0.1 * (a // PARTS_A)
+        if t == 0 and a < PARTS_A:
+            wait = PIECE * (PIECES + max(chips - 2, 0)) + HOP * (chips - 1) + step * (a - 1) + HOP
+            return max(stage_last - PIECE - HOP + 0.2, START + (wait if a else 0.0))
+        j = a % PARTS_A
+        place = PARTS_A + 1 + 2 * j + (1 if t else 0)
+        return START + PIECE * PIECES + step * place + 3.0 * HOP + 30.0 * max(t - 1, 0)
 
     for a, (j, second) in enumerate(order):
         for way in range(2):
@@ -479,61 +521,87 @@
             for d in range(chips):
                 time = 0.0
                 if d < chips - 1 and a >= d:
-                    time = PIECE * (PIECES - 1 + d) + HOP * d + 0.05 if d else 0.0
-                at(time, functools.partial(ring_own, j, hb, way, classes[way] == d, d == 0))
+                    time = START + PIECE * (PIECES - 1 + d) + HOP * d + 0.05 if d else 0.0
+                if a >= held_back:
+                    time = ring_time(a - held_back, 0) + 0.1
+                at(time, functools.partial(ring_own, j, hb, way, classes[way] == d))
             for t in range(reach):
                 if carried(way, hb, t):
-                    at(ring_time(a, t), functools.partial(ring_arrive, j, hb, way, t))
+                    forwards = t + 1 < reach and carried(way, hb, t + 1)
+                    at(ring_time(a, t) + (0.0 if forwards else 1.0),
+                       functools.partial(ring_arrive, j, hb, way, t), 0 if forwards else 1, 0.03)
+    for t in range(reach):
+        count = high if t < reach - 1 else high // 2
+        for way in range(2):
+            drain(ring_time(2 * PARTS_A - 1, t) + 4.0, out.at[pl.ds(0, count)], ("ring", way, t))
+            drain(ring_time(2 * PARTS_A - 1, t) + 8.0, out.at[pl.ds(0, count)], ("ringP", way, t))
 
     def own_pass(j):
         ref = colbuf[j].at[pl.ds(r * blocks, blocks)]
-        send(v.at[:, :, pl.ds(j * wide, wide)], ref, ("own", j), partner)
+        send(ref, ref, ("own",), ("tiles", j), partner)
+
+    def alpha_step(j):
+        ring_finish(j)
+        alpha_compute(j)
+        alphas.append(j)
+        if len(alphas) == PARTS_A:
+            for entry in held:
+                flush(*entry)
 
     for j in range(PARTS_A):
         at(0.5, functools.partial(own_pass, j))
-        done = max(ring_time(j, reach - 1), ring_time(PARTS_A + j, max(reach - 2, 0))) + 2.5
-        at(done, functools.partial(ring_finish, j))
-        at(done, functools.partial(alpha_compute, j))
+        done = max(ring_time(j, reach - 1), ring_time(PARTS_A + j, max(reach - 2, 0))) + 3.0
+        at(done, functools.partial(alpha_step, j), 4, 1.4)
+
+    drain(25.0, out, ("own",))
 
     def prepare():
         out[...] = jnp.zeros_like(out)
         gather_pairs()
-        wait_tab()
         widen(own_tab, 0, alpha_signs)
 
-    at(0.6, prepare)
-
-    groups = [[0], [1, 2], [3, 4], [5, 6, 7]]
+    at(0.6, prepare, 0, 4.0)
+
+    groups = [[0], [1, 2, 3, 4], [5, 6, 7]]
 
     def finish_time(i, t):
         k = max(k for k, chunk in enumerate(chunks) if chunk[0] == i)
-        return arrival(t, k, helps and k not in early) + 0.1
+        return START + arrival(t, k, helps and k not in early) + 0.1
+
+    def help_step(i):
+        line_finish(i)
+        help_beta(i)
+
+    def own_step(group, finish, cond):
+        if finish:
+            for i in group:
+                line_finish(i)
+        own_beta(group, cond)
+        flush(firsts[group[0]], sum(parts[i][0] for i in group), cond)
 
     for i, (height, helped) in enumerate(parts):
-        inside, outside = finish_time(i, max(cols - 3, 0)), finish_time(i, cols - 2)
         if helped:
-            inside = max(inside, help_ready) if i == 1 else inside
-            at(inside, functools.partial(line_finish, i))
-            at(inside, functools.partial(help_beta, i))
-            at(outside + 15.0 + i, functools.partial(take_sums, i))
-        else:
-            at(outside, functools.partial(line_finish, i))
+            ready = max(finish_time(i, max(cols - 3, 0)), help_ready)
+            at(ready, functools.partial(help_step, i), 2, 1.9)
+            at(ready + 11.0, functools.partial(take_sums, i), 5, 0.0)
+    if helps:
+        drain(help_ready + TILE, shared, ("sums",), lambda: helper)
     for group in groups:
         inside, outside = finish_time(group[-1], max(cols - 3, 0)), finish_time(group[-1], cols - 2)
         if parts[group[0]][1]:
-            at(max(inside, help_ready) + 0.1, functools.partial(own_beta, group, inner))
+            at(max(inside, help_ready) + 0.1, functools.partial(own_step, group, False, inner), 6, 2.6)
+        elif helps:
+            at(inside + 0.1, functools.partial(own_step, group, False, inner), 6, 2.6)
+            at(outside + 0.1, functools.partial(own_step, group, True, at_end), 6, 0.0)
         else:
-            at(outside + 0.1, functools.partial(own_beta, group, None))
-
-    for _, _, action in sorted(plan, key=lambda entry: entry[:2]):
+            at(outside + 0.1, functools.partial(own_step, group, True, None), 6, 2.6)
+
+    for action in in_order(plan):
         action()
-
-    for s in range(spread):
-        for h in range(2):
-            for q in range(PIECES):
-                table_drain(s, h, q)
-    for cond, copy in pending:
-        when(cond, copy.wait_send)
+    for wait in flushes:
+        wait()
+    assert len(numbers[0]) == ssem.shape[0] and len(numbers[1]) == rsem.shape[0]
+    assert len(local) <= lsem.shape[0]
 
 
 def local(vector, one_electron, links, counts, pairs, signs, rows, cols):
@@ -545,8 +613,12 @@
     parts = row_parts(high, cols)
     helped = sum(height for height, aided in parts if aided)
     reach = rows // 4
-    messages = rows - 1 + 2 * len(row_chunks(high, cols)) * (cols - 1)
-    messages += PARTS_A * (1 + 8 * reach) + spread * 2 * PIECES * 4 + len(parts)
+    sends = rows - 1 + 2 * (cols - 1) + 4 * reach + 2 + spread * 3
+    arrivals = rows - 1 + PARTS_A * (4 * reach - 1) + spread * (2 * PIECES + 1)
+    arrivals += sum(2 * (cols - 2 if chunk[4] else cols - 1) for chunk in row_chunks(high, cols))
+    if cols >= 4:
+        sends += 2 * (cols - 2) + spread * 2
+        arrivals += len(parts) - 1 + spread * (2 * PIECES + 1)
     scratch = [pltpu.VMEM((rows * blocks, size, width // PARTS_A), jnp.float32)] * PARTS_A
     scratch += [pltpu.VMEM((cols * blocks * spread, height, size), jnp.float32) for height, _ in parts]
     scratch += [
@@ -557,6 +629,7 @@
         pltpu.VMEM((spread * tables // 2, size, 2 * size), jnp.bfloat16),
         pltpu.VMEM((spread * tables // 2, size, 2 * size), jnp.bfloat16),
         pltpu.VMEM((max(helped, 8), width), jnp.float32),
+        pltpu.VMEM((high, width), jnp.float32),
         pltpu.VMEM((rows, blocks, link_max), jnp.int32),
         pltpu.SMEM((rows, blocks, link_max), jnp.int32),
         pltpu.SMEM((link_max, links.shape[0]), jnp.int32),
@@ -565,9 +638,9 @@
         pltpu.SMEM((blocks, link_max), jnp.float32),
         pltpu.SMEM((blocks * spread, link_max), jnp.float32),
         pltpu.SMEM((blocks * spread, link_max), jnp.float32),
-        pltpu.SemaphoreType.DMA((messages,)),
-        pltpu.SemaphoreType.DMA((messages,)),
-        pltpu.SemaphoreType.DMA((5 + len(parts) + PARTS_A + spread,)),
+        pltpu.SemaphoreType.DMA((sends,)),
+        pltpu.SemaphoreType.DMA((arrivals,)),
+        pltpu.SemaphoreType.DMA((8 + 2 * len(parts) + PARTS_A + spread,)),
     ]
     far = pl.BlockSpec(memory_space=pltpu.HBM)
     operands = (links.T, counts, one_electron, pairs, vector.reshape(blocks, size, width),
@@ -576,7 +649,7 @@
         functools.partial(kernel, rows, cols, blocks, link_max),
         out_shape=jax.ShapeDtypeStruct(vector.shape, jnp.float32),
         in_specs=[far] * 6,
-        out_specs=pl.BlockSpec(memory_space=pltpu.VMEM),
+        out_specs=pl.BlockSpec(memory_space=pl.ANY),
         scratch_shapes=scratch,
         compiler_params=pltpu.CompilerParams(
             collective_id=0, has_side_effects=True, vmem_limit_bytes=48 << 20),

time: 129 us -> 119 us (0.922)
  Pallas kernels: 127 us -> 117 us
    pallas_call x1, Pallas kernels: 127 us -> 117 us  [local(): pl.pallas_call(functools.partial(kernel, rows, cols, blocks, link_max), o...]
where the time goes in v3:
time: 119 us; the launch traced here: 118 us
  Pallas kernels  117 us (98%)
  local copies, waits for them, and re-layouts  1.32 us (1%)
    pallas_call x1, Pallas kernels, local(): pl.pallas_call(functools.partial(kernel, rows, cols, blocks, link_max), o...  117 us

profile of v3, /device:TPU:0, one launch (start us, length us, event | category | flops | bytes accessed | tf_op | source)
XLA Modules:
  0.0 118.5 jit_solution(14650880115925951493)
XLA Ops:
  0.0 117.2 %shard_map.64 = f32[512,1024]{1,0:T(8,128)S(1)} custom-call(s32[8,32]{1,0:T(8,128)} %bitcast.5, s32[32]{0:T(128)} %counts_in.1, f32[16,16]{1,0:T(8,128)} %integrals_in.1, s32[4,8]{1,0:T(4,128)} %pairs.1, f32[4,128,1024]{2,1,0:T(8,128)} %bitcast.3, s32[32,128,128]{2,1,0:T(8,128)} %bitcast.4), custom_call_target="tpu_custom_call" | custom-call | tf_op jit(solution)/shard_map/pallas_call | solution.py:648
  117.2 1.3 %copy.8 = f32[512,1024]{1,0:T(8,128)} copy(f32[512,1024]{1,0:T(8,128)S(1)} %shard_map.64) | data formatting | bytes 4194304

commit v4 on v3

--- a/solution.py
+++ b/solution.py
@@ -11,6 +11,8 @@
 PARTS_A = 4
 PIECES = 4
 START = 4.5
+LEAD = 2.5
+SLACK = 0.7
 TILE = 45.0
 HOP = 1.5
 PIECE = 5.6
@@ -39,11 +41,21 @@
 
 def in_order(plan):
     left = sorted(enumerate(plan), key=lambda entry: (entry[1][0], entry[0]))
+    urgent = [entry for entry in left if entry[1][1] <= 2]
     now, result = 0.0, []
     while left:
-        ready = [entry for entry in left if entry[1][0] <= now] or [left[0]]
+        ready = [entry for entry in left if entry[1][0] <= now]
+        soon = [entry for entry in urgent if entry[1][0] > now][:1]
+        if soon:
+            room = soon[0][1][0] - now + SLACK
+            ready = [entry for entry in ready if entry[1][1] <= 2 or entry[1][2] <= room]
+        if not ready:
+            now = min(entry[1][0] for entry in (soon or left))
+            ready = [entry for entry in left if entry[1][0] <= now and entry[1][1] <= 2] or left[:1]
         chosen = min(ready, key=lambda entry: (entry[1][1], entry[1][0], entry[0]))
         left.remove(chosen)
+        if chosen[1][1] <= 2:
+            urgent.remove(chosen)
         start, _, length, action = chosen[1]
         now = max(now, start) + length
         result.append(action)
@@ -445,7 +457,8 @@
             for t in range(cols - 1):
                 for edge in (False, True):
                     late = edge and late_k
-                    at(START + arrival(t, k, late), functools.partial(line_arrive, k, way, t, edge, True))
+                    at(START - LEAD + arrival(t, k, late) + (1.5 if t else 0.0),
+                       functools.partial(line_arrive, k, way, t, edge, True))
 
     for helped in (False, True) if helps else (False,):
         count = sum(height for height, aided_part in parts if aided_part == helped)
@@ -562,7 +575,7 @@
 
     at(0.6, prepare, 0, 4.0)
 
-    groups = [[0], [1, 2, 3, 4], [5, 6, 7]]
+    groups = [[0], [1, 2], [3, 4], [5, 6, 7]]
 
     def finish_time(i, t):
         k = max(k for k, chunk in enumerate(chunks) if chunk[0] == i)
@@ -640,7 +653,7 @@
         pltpu.SMEM((blocks * spread, link_max), jnp.float32),
         pltpu.SemaphoreType.DMA((sends,)),
         pltpu.SemaphoreType.DMA((arrivals,)),
-        pltpu.SemaphoreType.DMA((8 + 2 * len(parts) + PARTS_A + spread,)),
+        pltpu.SemaphoreType.DMA((8 + 3 * len(parts) + PARTS_A + spread,)),
     ]
     far = pl.BlockSpec(memory_space=pltpu.HBM)
     operands = (links.T, counts, one_electron, pairs, vector.reshape(blocks, size, width),

time: 119 us -> 115 us (0.966)
  Pallas kernels: 117 us -> 113 us
    pallas_call x1, Pallas kernels: 117 us -> 113 us  [local(): pl.pallas_call(functools.partial(kernel, rows, cols, blocks, link_max), o...]
where the time goes in v4:
time: 115 us
  Pallas kernels  113 us (98%)
  local copies, waits for them, and re-layouts  1.32 us (1%)
    pallas_call x1, Pallas kernels, local(): pl.pallas_call(functools.partial(kernel, rows, cols, blocks, link_max), o...  113 us

profile of v4, /device:TPU:0, one launch (start us, length us, event | category | flops | bytes accessed | tf_op | source)
XLA Modules:
  0.0 114.7 jit_solution(7815946503643459263)
XLA Ops:
  0.0 113.3 %shard_map.64 = f32[512,1024]{1,0:T(8,128)S(1)} custom-call(s32[8,32]{1,0:T(8,128)} %bitcast.5, s32[32]{0:T(128)} %counts_in.1, f32[16,16]{1,0:T(8,128)} %integrals_in.1, s32[4,8]{1,0:T(4,128)} %pairs.1, f32[4,128,1024]{2,1,0:T(8,128)} %bitcast.3, s32[32,128,128]{2,1,0:T(8,128)} %bitcast.4), custom_call_target="tpu_custom_call" | custom-call | tf_op jit(solution)/shard_map/pallas_call | solution.py:661
  113.3 1.3 %copy.8 = f32[512,1024]{1,0:T(8,128)} copy(f32[512,1024]{1,0:T(8,128)S(1)} %shard_map.64) | data formatting | bytes 4194304

commit v5 on v4

--- a/solution.py
+++ b/solution.py
@@ -26,7 +26,7 @@
 
 def row_parts(high, cols):
     helps = cols >= 4
-    return [(high // 4, False)] + [(high // 8, helps)] * 5 + [(high // 16, helps)] * 2
+    return [(high // 4, False)] * 2 + [(high // 16, helps)] * 7 + [(high // 32, helps)] * 2
 
 
 def row_chunks(high, cols):
@@ -343,25 +343,34 @@
         if helps:
             coefficients(help_coef, aided * blocks_b, blocks_b)
 
+    def trips(first, last, body):
+        together = max(u for u in (4, 2, 1) if (last - first) % u == 0)
+
+        @pl.loop(0, (last - first) // together)
+        def _(trip):
+            for turn in range(together):
+                body(first + trip * together + turn)
+
     def alpha_compute(j):
-        @pl.loop(0, blocks)
-        def _(block):
-            total = jnp.zeros((size, wide), jnp.float32)
+        def body(block):
+            total = None
             for l in range(link_max):
                 source = links[l, r * blocks + block]
                 up_part, low_part = split(colbuf[j][source] * alpha_coef[block, l])
-                total = total + jnp.dot(
+                term = jnp.dot(
                     alpha_signs[block * link_max + l], jnp.concatenate([up_part, low_part], axis=0),
                     preferred_element_type=jnp.float32)
+                total = term if total is None else total + term
             where = (pl.ds(pl.multiple_of(block * size, size), size), pl.ds(j * wide, wide))
             out[where] = out[where] + total
 
-    def beta_compute(group, owner, coef, signs, target, start, add):
+        trips(0, blocks, body)
+
+    def beta_compute(group, owner, coef, signs, target, start, add, span=None):
         count = sum(parts[i][0] for i in group)
 
-        @pl.loop(0, blocks_b)
-        def _(block):
-            total = jnp.zeros((2 * count, size), jnp.float32)
+        def body(block):
+            total = None
             for l in range(0, link_max, 2):
                 highs, lows = [], []
                 for m in (l, l + 1):
@@ -372,20 +381,23 @@
                     lows.append(low_part)
                 value = jnp.concatenate(
                     [jnp.concatenate(highs, axis=1), jnp.concatenate(lows, axis=1)], axis=0)
-                total = total + lax.dot_general(
+                term = lax.dot_general(
                     value, signs[block * (link_max // 2) + l // 2],
                     (((1,), (1,)), ((), ())), preferred_element_type=jnp.float32)
+                total = term if total is None else total + term
             total = total[:count] + total[count:]
             where = (pl.ds(start, count), pl.ds(pl.multiple_of(block * size, size), size))
             if add:
                 total = target[where] + total
             target[where] = total
 
+        trips(*(span or (0, blocks_b)), body)
+
     shared_first = sum(height for height, helped in parts if not helped)
 
-    def own_beta(group, cond):
+    def own_beta(group, cond, span):
         def action():
-            beta_compute(group, c, beta_coef, beta_signs, out, firsts[group[0]], True)
+            beta_compute(group, c, beta_coef, beta_signs, out, firsts[group[0]], True, span)
         when(cond, action)
 
     def help_beta(i):
@@ -563,8 +575,8 @@
 
     for j in range(PARTS_A):
         at(0.5, functools.partial(own_pass, j))
-        done = max(ring_time(j, reach - 1), ring_time(PARTS_A + j, max(reach - 2, 0))) + 3.0
-        at(done, functools.partial(alpha_step, j), 4, 1.4)
+        done = max(ring_time(j, reach - 1), ring_time(PARTS_A + j, max(reach - 2, 0))) + 4.5
+        at(done, functools.partial(alpha_step, j), 4, 0.9)
 
     drain(25.0, out, ("own",))
 
@@ -575,39 +587,42 @@
 
     at(0.6, prepare, 0, 4.0)
 
-    groups = [[0], [1, 2], [3, 4], [5, 6, 7]]
+    groups = [[0, 1], [2, 3, 4, 5], [6, 7, 8, 9, 10]]
 
     def finish_time(i, t):
         k = max(k for k, chunk in enumerate(chunks) if chunk[0] == i)
-        return START + arrival(t, k, helps and k not in early) + 0.1
+        return START - LEAD + 1.0 + arrival(t, k, helps and k not in early)
 
     def help_step(i):
         line_finish(i)
         help_beta(i)
 
-    def own_step(group, finish, cond):
-        if finish:
+    def own_step(group, finish, cond, turn=0, turns=1):
+        if finish and not turn:
             for i in group:
                 line_finish(i)
-        own_beta(group, cond)
-        flush(firsts[group[0]], sum(parts[i][0] for i in group), cond)
+        span = (blocks_b * turn // turns, blocks_b * (turn + 1) // turns)
+        own_beta(group, cond, span)
+        if turn == turns - 1:
+            flush(firsts[group[0]], sum(parts[i][0] for i in group), cond)
 
     for i, (height, helped) in enumerate(parts):
         if helped:
             ready = max(finish_time(i, max(cols - 3, 0)), help_ready)
-            at(ready, functools.partial(help_step, i), 2, 1.9)
+            at(ready, functools.partial(help_step, i), 2, 1.0)
             at(ready + 11.0, functools.partial(take_sums, i), 5, 0.0)
     if helps:
         drain(help_ready + TILE, shared, ("sums",), lambda: helper)
     for group in groups:
         inside, outside = finish_time(group[-1], max(cols - 3, 0)), finish_time(group[-1], cols - 2)
-        if parts[group[0]][1]:
-            at(max(inside, help_ready) + 0.1, functools.partial(own_step, group, False, inner), 6, 2.6)
-        elif helps:
-            at(inside + 0.1, functools.partial(own_step, group, False, inner), 6, 2.6)
+        if not helps:
+            at(outside + 0.1, functools.partial(own_step, group, True, None), 6, 2.6)
+            continue
+        for turn in range(2):
+            at(max(inside, help_ready if parts[group[0]][1] else 0.0) + 0.1 + 0.01 * turn,
+               functools.partial(own_step, group, False, inner, turn, 2), 6, 0.9)
+        if not parts[group[0]][1]:
             at(outside + 0.1, functools.partial(own_step, group, True, at_end), 6, 0.0)
-        else:
-            at(outside + 0.1, functools.partial(own_step, group, True, None), 6, 2.6)
 
     for action in in_order(plan):
         action()
@@ -631,7 +646,7 @@
     arrivals += sum(2 * (cols - 2 if chunk[4] else cols - 1) for chunk in row_chunks(high, cols))
     if cols >= 4:
         sends += 2 * (cols - 2) + spread * 2
-        arrivals += len(parts) - 1 + spread * (2 * PIECES + 1)
+        arrivals += sum(1 for _, aided in parts if aided) + spread * (2 * PIECES + 1)
     scratch = [pltpu.VMEM((rows * blocks, size, width // PARTS_A), jnp.float32)] * PARTS_A
     scratch += [pltpu.VMEM((cols * blocks * spread, height, size), jnp.float32) for height, _ in parts]
     scratch += [

time: 115 us -> 111 us (0.965)
  Pallas kernels: 113 us -> 109 us
    pallas_call x1, Pallas kernels: 113 us -> 109 us  [local(): pl.pallas_call(functools.partial(kernel, rows, cols, blocks, link_max), o...]
where the time goes in v5:
time: 111 us
  Pallas kernels  109 us (98%)
  local copies, waits for them, and re-layouts  1.32 us (1%)
    pallas_call x1, Pallas kernels, local(): pl.pallas_call(functools.partial(kernel, rows, cols, blocks, link_max), o...  109 us

profile of v5, /device:TPU:0, one launch (start us, length us, event | category | flops | bytes accessed | tf_op | source)
XLA Modules:
  0.0 110.8 jit_solution(11728522717945491232)
XLA Ops:
  0.0 109.5 %shard_map.64 = f32[512,1024]{1,0:T(8,128)S(1)} custom-call(s32[8,32]{1,0:T(8,128)} %bitcast.5, s32[32]{0:T(128)} %counts_in.1, f32[16,16]{1,0:T(8,128)} %integrals_in.1, s32[4,8]{1,0:T(4,128)} %pairs.1, f32[4,128,1024]{2,1,0:T(8,128)} %bitcast.3, s32[32,128,128]{2,1,0:T(8,128)} %bitcast.4), custom_call_target="tpu_custom_call" | custom-call | tf_op jit(solution)/shard_map/pallas_call | solution.py:676
  109.5 1.3 %copy.8 = f32[512,1024]{1,0:T(8,128)} copy(f32[512,1024]{1,0:T(8,128)S(1)} %shard_map.64) | data formatting | bytes 4194304

commit v6 on v5

--- a/solution.py
+++ b/solution.py
@@ -12,7 +12,7 @@
 PIECES = 4
 START = 4.5
 LEAD = 2.5
-SLACK = 0.7
+SLACK = 0.3
 TILE = 45.0
 HOP = 1.5
 PIECE = 5.6
@@ -26,7 +26,7 @@
 
 def row_parts(high, cols):
     helps = cols >= 4
-    return [(high // 4, False)] * 2 + [(high // 16, helps)] * 7 + [(high // 32, helps)] * 2
+    return [(high // 4, False)] * 2 + [(high // 32, helps)] * 16
 
 
 def row_chunks(high, cols):
@@ -170,21 +170,25 @@
     wait_small = [load(pairs, pairs_v.at[r]), load(links_in, links), load(counts_in, counts),
                   load(integrals_in, integrals)]
 
-    def load_rows(i):
+    def load_rows(group):
         sem = lsem.at[len(local)]
-        first = firsts[i]
-        for k in range(blocks_b):
-            pltpu.make_async_copy(
-                v.at[first // size, pl.ds(first % size, parts[i][0]), pl.ds(k * size, size)],
-                rowbuf[i].at[c * blocks_b + k], sem).start()
-        ref = rowbuf[i].at[pl.ds(c * blocks_b, blocks_b)]
+        for i in group:
+            first = firsts[i]
+            for k in range(blocks_b):
+                pltpu.make_async_copy(
+                    v.at[first // size, pl.ds(first % size, parts[i][0]), pl.ds(k * size, size)],
+                    rowbuf[i].at[c * blocks_b + k], sem).start()
+        ref = out.at[pl.ds(0, sum(parts[i][0] for i in group))]
         local.append(pltpu.make_async_copy(ref, ref, sem))
         return local[-1].wait
 
-    wait_rows = [load_rows(i) for i in range(len(parts))]
+    wait_rows = {group[0]: load_rows(group) for group in ([0], [1], range(2, len(parts)))}
     wait_tab = load(tab, own_tab)
-    wait_cols = [load(v.at[:, :, pl.ds(j * wide, wide)], colbuf[j].at[pl.ds(r * blocks, blocks)])
-                 for j in range(PARTS_A)]
+    for j in range(PARTS_A):
+        pltpu.make_async_copy(v.at[:, :, pl.ds(j * wide, wide)], colbuf[j].at[pl.ds(r * blocks, blocks)],
+                              lsem.at[len(local)]).start()
+    local.append(pltpu.make_async_copy(out, out, lsem.at[len(local)]))
+    wait_cols = local[-1].wait
 
     pl.semaphore_wait(barrier, rows - 1 + has_up.astype(jnp.int32) + has_down.astype(jnp.int32))
 
@@ -203,6 +207,9 @@
         length = TILE * chunks[k][2] / high
         return ends(k) + TILE * tiles + HOP + (length + HOP) * (t if late else max(t - far, 0))
 
+    def line_key(k, way, t):
+        return "line", k, way * (1 + t) % cols
+
     def row_chunk(k, tile):
         part, offset, count, _, _ = chunks[k]
         return rowbuf[part].at[pl.ds(tile * blocks_b, blocks_b), pl.ds(offset, count), :]
@@ -212,7 +219,7 @@
         position = c if way == 1 else cols - 1 - c
         limit = cols - 2 if helped else cols - 1
         ref = row_chunk(k, c)
-        send(ref, ref, ("line", way, 0, helped), ("line", way, k, 0), reach_up[way], cond & (position < limit))
+        send(ref, ref, ("line", way, 0, helped), line_key(k, way, 0), reach_up[way], cond & (position < limit))
 
     def line_arrive(k, way, t, edge, forward):
         helped = chunks[k][4]
@@ -223,9 +230,9 @@
         position = c if way == 1 else cols - 1 - c
         cond = position == t + 1 if edge else (position > t + 1) & (position <= last)
         ref = row_chunk(k, jnp.clip(c - way * (1 + t), 0, cols - 1))
-        arrive(ref, ("line", way, k, t), cond)
+        arrive(ref, line_key(k, way, t), cond)
         if onward:
-            send(ref, ref, ("line", way, t + 1, helped), ("line", way, k, t + 1), reach_up[way],
+            send(ref, ref, ("line", way, t + 1, helped), line_key(k, way, t + 1), reach_up[way],
                  cond if edge else cond & (position < last))
 
     def line_finish(i):
@@ -256,12 +263,12 @@
         ref = beta_tab.at[s, part]
         src = ref if d else own_tab.at[part]
         if d:
-            arrive(ref, ("table", s, h, q), here)
+            arrive(ref, ("table", s // 2, h, q), here)
         if d + 1 < chips:
-            send(src, ref, ("table", s, h), ("table", s, h, q), ring[h], here)
+            send(src, ref, ("table", s, h), ("table", s // 2, h, q), ring[h], here)
         send(src, ref, ("tableP", s), ("tableP", s), partner, here)
         if helps:
-            send(src, help_tab.at[s, part], ("help", s), ("help", s, h, q), inward, here & at_end)
+            send(src, help_tab.at[s, part], ("help", s), ("help", s // 2, h, q), inward, here & at_end)
 
     def table_finish():
         for s in range(spread):
@@ -273,7 +280,7 @@
         source_core = table_places(s)[0]
         aided_core = lax.rem(aided * spread + s, 2)
         ref = help_tab.at[s, table_part(h, q)]
-        arrive(ref, ("help", s, h, q), helper & (core == aided_core))
+        arrive(ref, ("help", s // 2, h, q), helper & (core == aided_core))
         send(ref, ref, ("helpP", s), ("helpP", s), partner, helper & (core == aided_core))
 
     def help_finish():
@@ -400,17 +407,20 @@
             beta_compute(group, c, beta_coef, beta_signs, out, firsts[group[0]], True, span)
         when(cond, action)
 
+    def sums_key(i):
+        return line_key(next(k for k, chunk in enumerate(chunks) if chunk[0] == i), 1, 0)
+
     def help_beta(i):
         @pl.when(helper)
         def _():
             beta_compute([i], aided, help_coef, help_signs, shared, firsts[i] - shared_first, False)
 
         ref = shared.at[pl.ds(firsts[i] - shared_first, parts[i][0])]
-        send(ref, ref, ("sums",), ("sums", i), (r, aided), helper)
+        send(ref, ref, ("sums",), sums_key(i), (r, aided), helper)
 
     def take_sums(i):
         ref = shared.at[pl.ds(firsts[i] - shared_first, parts[i][0])]
-        arrive(ref, ("sums", i), at_end)
+        arrive(ref, sums_key(i), at_end)
 
         @pl.when(at_end)
         def _():
@@ -419,21 +429,21 @@
 
         flush(firsts[i], parts[i][0], at_end)
 
-    flushes, held, alphas = [], [], []
+    held, alphas = [], []
 
     def flush(first, count, cond):
         if len(alphas) < PARTS_A:
             held.append((first, count, cond))
             return
         where = pl.ds(first, count)
-        flushes.append(load(out.at[where], result.at[where], cond))
+        when(cond, pltpu.make_async_copy(out.at[where], result.at[where], lsem.at[lsem.shape[0] - 1]).start)
 
     table_loads = []
 
     def begin():
         always = jnp.bool_(True)
         for k in range(len(chunks)):
-            if chunks[k][1] == 0:
+            if chunks[k][1] == 0 and chunks[k][0] in wait_rows:
                 wait_rows[chunks[k][0]]()
             first = k in early or not helps
             line_own(k, 1, always if first else has_down)
@@ -446,8 +456,7 @@
             table_loads.append(load(tab, beta_tab.at[s], (core == source_core) & (hops[0] == 0)))
 
     def begin_tiles():
-        for j in range(PARTS_A):
-            wait_cols[j]()
+        wait_cols()
 
     at(-4.0, begin)
     at(-2.0, begin_tables)
@@ -587,7 +596,7 @@
 
     at(0.6, prepare, 0, 4.0)
 
-    groups = [[0, 1], [2, 3, 4, 5], [6, 7, 8, 9, 10]]
+    groups = [[0], [1], list(range(2, 10)), list(range(10, 18))]
 
     def finish_time(i, t):
         k = max(k for k, chunk in enumerate(chunks) if chunk[0] == i)
@@ -609,7 +618,7 @@
     for i, (height, helped) in enumerate(parts):
         if helped:
             ready = max(finish_time(i, max(cols - 3, 0)), help_ready)
-            at(ready, functools.partial(help_step, i), 2, 1.0)
+            at(ready + 1.5, functools.partial(help_step, i), 2, 0.85)
             at(ready + 11.0, functools.partial(take_sums, i), 5, 0.0)
     if helps:
         drain(help_ready + TILE, shared, ("sums",), lambda: helper)
@@ -619,17 +628,16 @@
             at(outside + 0.1, functools.partial(own_step, group, True, None), 6, 2.6)
             continue
         for turn in range(2):
-            at(max(inside, help_ready if parts[group[0]][1] else 0.0) + 0.1 + 0.01 * turn,
-               functools.partial(own_step, group, False, inner, turn, 2), 6, 0.9)
+            at((max(inside, help_ready) + 1.6 if parts[group[0]][1] else inside + 0.1) + 0.01 * turn,
+               functools.partial(own_step, group, False, inner, turn, 2), 6, 0.8)
         if not parts[group[0]][1]:
             at(outside + 0.1, functools.partial(own_step, group, True, at_end), 6, 0.0)
 
     for action in in_order(plan):
         action()
-    for wait in flushes:
-        wait()
+    pltpu.make_async_copy(out, result, lsem.at[lsem.shape[0] - 1]).wait()
     assert len(numbers[0]) == ssem.shape[0] and len(numbers[1]) == rsem.shape[0]
-    assert len(local) <= lsem.shape[0]
+    assert len(local) == lsem.shape[0] - 1
 
 
 def local(vector, one_electron, links, counts, pairs, signs, rows, cols):
@@ -642,11 +650,11 @@
     helped = sum(height for height, aided in parts if aided)
     reach = rows // 4
     sends = rows - 1 + 2 * (cols - 1) + 4 * reach + 2 + spread * 3
-    arrivals = rows - 1 + PARTS_A * (4 * reach - 1) + spread * (2 * PIECES + 1)
-    arrivals += sum(2 * (cols - 2 if chunk[4] else cols - 1) for chunk in row_chunks(high, cols))
+    pieces = 2 * PIECES * ((spread + 1) // 2) + spread
+    arrivals = rows - 1 + PARTS_A * (4 * reach - 1) + pieces + len(row_chunks(high, cols)) * (cols - 1)
     if cols >= 4:
         sends += 2 * (cols - 2) + spread * 2
-        arrivals += sum(1 for _, aided in parts if aided) + spread * (2 * PIECES + 1)
+        arrivals += pieces
     scratch = [pltpu.VMEM((rows * blocks, size, width // PARTS_A), jnp.float32)] * PARTS_A
     scratch += [pltpu.VMEM((cols * blocks * spread, height, size), jnp.float32) for height, _ in parts]
     scratch += [
@@ -668,7 +676,7 @@
         pltpu.SMEM((blocks * spread, link_max), jnp.float32),
         pltpu.SemaphoreType.DMA((sends,)),
         pltpu.SemaphoreType.DMA((arrivals,)),
-        pltpu.SemaphoreType.DMA((8 + 3 * len(parts) + PARTS_A + spread,)),
+        pltpu.SemaphoreType.DMA((10 + spread,)),
     ]
     far = pl.BlockSpec(memory_space=pltpu.HBM)
     operands = (links.T, counts, one_electron, pairs, vector.reshape(blocks, size, width),

time: 111 us -> 110 us (level)
    pallas_call x1, Pallas kernels: 109 us -> 108 us  [local(): pl.pallas_call(functools.partial(kernel, rows, cols, blocks, link_max), o...]
where the time goes in v6:
time: 110 us
  Pallas kernels  108 us (98%)
  local copies, waits for them, and re-layouts  1.32 us (1%)
    pallas_call x1, Pallas kernels, local(): pl.pallas_call(functools.partial(kernel, rows, cols, blocks, link_max), o...  108 us

profile of v6, /device:TPU:0, one launch (start us, length us, event | category | flops | bytes accessed | tf_op | source)
XLA Modules:
  0.0 109.6 jit_solution(15218159540236401799)
XLA Ops:
  0.0 108.3 %shard_map.64 = f32[512,1024]{1,0:T(8,128)S(1)} custom-call(s32[8,32]{1,0:T(8,128)} %bitcast.5, s32[32]{0:T(128)} %counts_in.1, f32[16,16]{1,0:T(8,128)} %integrals_in.1, s32[4,8]{1,0:T(4,128)} %pairs.1, f32[4,128,1024]{2,1,0:T(8,128)} %bitcast.3, s32[32,128,128]{2,1,0:T(8,128)} %bitcast.4), custom_call_target="tpu_custom_call" | custom-call | tf_op jit(solution)/shard_map/pallas_call | solution.py:684
  108.3 1.3 %copy.8 = f32[512,1024]{1,0:T(8,128)} copy(f32[512,1024]{1,0:T(8,128)S(1)} %shard_map.64) | data formatting | bytes 4194304

commit v7 on v6

--- a/solution.py
+++ b/solution.py
@@ -12,7 +12,7 @@
 PIECES = 4
 START = 4.5
 LEAD = 2.5
-SLACK = 0.3
+SLACK = 0.1
 TILE = 45.0
 HOP = 1.5
 PIECE = 5.6
@@ -26,7 +26,7 @@
 
 def row_parts(high, cols):
     helps = cols >= 4
-    return [(high // 4, False)] * 2 + [(high // 32, helps)] * 16
+    return [(high // 4, False)] * 2 + [(high // 16, False)] + [(high // 32, helps)] * 14
 
 
 def row_chunks(high, cols):
@@ -85,7 +85,7 @@
     half = blocks // 2
     piece = tables // (2 * PIECES)
     helps = cols >= 4
-    early = [k for k, chunk in enumerate(chunks) if chunk[0] < 2]
+    early = [k for k, chunk in enumerate(chunks) if chunk[0] < 3]
 
     r = lax.axis_index("row")
     c = lax.axis_index("col")
@@ -467,7 +467,7 @@
             line_own(k, 1, c == 0)
             line_own(k, -1, c == cols - 1)
 
-    stage_last = START + PIECE * (PIECES - 1 + chips - 1) + HOP * (chips - 1)
+    stage_last = START + PIECE * (PIECES - 1 + chips - 1) + HOP * (chips - 1) + 3.5
     if helps:
         at(stage_last + 0.1, rest)
 
@@ -498,7 +498,7 @@
         for h in range(2):
             for s in range(spread):
                 for d in range(chips):
-                    time = -1.0 if d == 0 else START + PIECE * (q + d) + HOP * d
+                    time = -1.0 if d == 0 else START + PIECE * (q + d) + HOP * d + (3.5 if d > 1 else 0.0)
                     at(time, functools.partial(table_stage, s, h, q, d))
     for s in range(spread):
         def mine(s=s):
@@ -528,7 +528,10 @@
         at(help_ready + 0.1, lambda: pl.when(helper)(lambda: couple_all(help_tab, help_signs)), 1, 1.0)
         help_ready += 0.2
 
-    order = [(j, second) for second in range(2) for j in range(PARTS_A)]
+    order = [(0, 0), (1, 0), (0, 1), (1, 1), (2, 0), (3, 0), (2, 1), (3, 1)]
+    own_place = dict(zip(order, (1, 2, 3, 4, 7, 8, 9, 11)))
+    passed_place = (5, 6, 10, 12)
+    held_back = {(2, 0): 1, (3, 0): 1, (2, 1): 1, (3, 1): 2}
     step = TILE / (2 * PARTS_A)
 
     classes = []
@@ -539,14 +542,12 @@
             kind = jnp.where(core == source_core, hops[h], kind)
         classes.append(kind)
 
-    held_back = PARTS_A + 1
-
-    def ring_time(a, t):
-        if t == 0 and a < PARTS_A:
-            wait = PIECE * (PIECES + max(chips - 2, 0)) + HOP * (chips - 1) + step * (a - 1) + HOP
-            return max(stage_last - PIECE - HOP + 0.2, START + (wait if a else 0.0))
-        j = a % PARTS_A
-        place = PARTS_A + 1 + 2 * j + (1 if t else 0)
+    def ring_time(j, second, t):
+        place = passed_place[j] if t else own_place[j, second]
+        if place == 1:
+            return stage_last - PIECE - HOP + 0.2
+        if place == 2:
+            return START + PIECE * (PIECES + max(chips - 2, 0)) + HOP * chips
         return START + PIECE * PIECES + step * place + 3.0 * HOP + 30.0 * max(t - 1, 0)
 
     for a, (j, second) in enumerate(order):
@@ -554,21 +555,21 @@
             hb = (1 - way) if second else way
             for d in range(chips):
                 time = 0.0
-                if d < chips - 1 and a >= d:
-                    time = START + PIECE * (PIECES - 1 + d) + HOP * d + 0.05 if d else 0.0
-                if a >= held_back:
-                    time = ring_time(a - held_back, 0) + 0.1
+                if d < chips - 1 and a >= d + min(d, 1):
+                    time = START + PIECE * (PIECES - 1 + d) + HOP * d + (3.55 if d > 1 else 0.05) if d else 0.0
+                if (j, second) in held_back:
+                    time = ring_time(held_back[j, second], 0, 0) + 0.1
                 at(time, functools.partial(ring_own, j, hb, way, classes[way] == d))
             for t in range(reach):
                 if carried(way, hb, t):
                     forwards = t + 1 < reach and carried(way, hb, t + 1)
-                    at(ring_time(a, t) + (0.0 if forwards else 1.0),
+                    at(ring_time(j, second, t) + (0.0 if forwards else 1.0),
                        functools.partial(ring_arrive, j, hb, way, t), 0 if forwards else 1, 0.03)
     for t in range(reach):
         count = high if t < reach - 1 else high // 2
         for way in range(2):
-            drain(ring_time(2 * PARTS_A - 1, t) + 4.0, out.at[pl.ds(0, count)], ("ring", way, t))
-            drain(ring_time(2 * PARTS_A - 1, t) + 8.0, out.at[pl.ds(0, count)], ("ringP", way, t))
+            drain(ring_time(PARTS_A - 1, 1, t) + 4.0, out.at[pl.ds(0, count)], ("ring", way, t))
+            drain(ring_time(PARTS_A - 1, 1, t) + 8.0, out.at[pl.ds(0, count)], ("ringP", way, t))
 
     def own_pass(j):
         ref = colbuf[j].at[pl.ds(r * blocks, blocks)]
@@ -584,7 +585,7 @@
 
     for j in range(PARTS_A):
         at(0.5, functools.partial(own_pass, j))
-        done = max(ring_time(j, reach - 1), ring_time(PARTS_A + j, max(reach - 2, 0))) + 4.5
+        done = max(ring_time(j, 0, reach - 1), ring_time(j, 1, max(reach - 2, 0))) + (2.5 if j < 2 else 4.5)
         at(done, functools.partial(alpha_step, j), 4, 0.9)
 
     drain(25.0, out, ("own",))
@@ -596,7 +597,7 @@
 
     at(0.6, prepare, 0, 4.0)
 
-    groups = [[0], [1], list(range(2, 10)), list(range(10, 18))]
+    groups = [[0], [1, 2], list(range(3, 10)), list(range(10, 17))]
 
     def finish_time(i, t):
         k = max(k for k, chunk in enumerate(chunks) if chunk[0] == i)

time: 110 us -> 109 us (level)
  no operation moved by 1% of the time
where the time goes in v7:
time: 109 us
  Pallas kernels  108 us (99%)
  local copies, waits for them, and re-layouts  1.32 us (1%)
    pallas_call x1, Pallas kernels, local(): pl.pallas_call(functools.partial(kernel, rows, cols, blocks, link_max), o...  108 us

profile of v7, /device:TPU:0, one launch (start us, length us, event | category | flops | bytes accessed | tf_op | source)
XLA Modules:
  0.0 109.2 jit_solution(4941557680751062738)
XLA Ops:
  0.0 107.9 %shard_map.64 = f32[512,1024]{1,0:T(8,128)S(1)} custom-call(s32[8,32]{1,0:T(8,128)} %bitcast.5, s32[32]{0:T(128)} %counts_in.1, f32[16,16]{1,0:T(8,128)} %integrals_in.1, s32[4,8]{1,0:T(4,128)} %pairs.1, f32[4,128,1024]{2,1,0:T(8,128)} %bitcast.3, s32[32,128,128]{2,1,0:T(8,128)} %bitcast.4), custom_call_target="tpu_custom_call" | custom-call | tf_op jit(solution)/shard_map/pallas_call | solution.py:685
  107.9 1.3 %copy.8 = f32[512,1024]{1,0:T(8,128)} copy(f32[512,1024]{1,0:T(8,128)S(1)} %shard_map.64) | data formatting | bytes 4194304

commit v8 on v7

--- a/solution.py
+++ b/solution.py
@@ -548,7 +548,7 @@
             return stage_last - PIECE - HOP + 0.2
         if place == 2:
             return START + PIECE * (PIECES + max(chips - 2, 0)) + HOP * chips
-        return START + PIECE * PIECES + step * place + 3.0 * HOP + 30.0 * max(t - 1, 0)
+        return START + PIECE * PIECES + step * place + (3.0 if place < 12 else 1.5) * HOP + 30.0 * max(t - 1, 0)
 
     for a, (j, second) in enumerate(order):
         for way in range(2):

time: 109 us -> 109 us (level)
  no operation moved by 1% of the time
where the time goes in v8:
time: 109 us
  Pallas kernels  108 us (99%)
  local copies, waits for them, and re-layouts  1.32 us (1%)
    pallas_call x1, Pallas kernels, local(): pl.pallas_call(functools.partial(kernel, rows, cols, blocks, link_max), o...  108 us

profile of v8, /device:TPU:0, one launch (start us, length us, event | category | flops | bytes accessed | tf_op | source)
XLA Modules:
  0.0 109.2 jit_solution(15574690150476503257)
XLA Ops:
  0.0 107.9 %shard_map.64 = f32[512,1024]{1,0:T(8,128)S(1)} custom-call(s32[8,32]{1,0:T(8,128)} %bitcast.5, s32[32]{0:T(128)} %counts_in.1, f32[16,16]{1,0:T(8,128)} %integrals_in.1, s32[4,8]{1,0:T(4,128)} %pairs.1, f32[4,128,1024]{2,1,0:T(8,128)} %bitcast.3, s32[32,128,128]{2,1,0:T(8,128)} %bitcast.4), custom_call_target="tpu_custom_call" | custom-call | tf_op jit(solution)/shard_map/pallas_call | solution.py:685
  107.9 1.3 %copy.8 = f32[512,1024]{1,0:T(8,128)} copy(f32[512,1024]{1,0:T(8,128)S(1)} %shard_map.64) | data formatting | bytes 4194304
